TPU v7x, 128 devices: a whole 4x4x4 slice. The times are simulated.
128 devices in a mesh: row: 8 (over z, core), col: 16 (over x, y).
Axes of the slice: x: 4, y: 4, z: 4, core: 2. Of those that a mesh axis runs over, the one named last changes fastest.
Arguments:
- features: bfloat16 [262144, 256], P(('row', 'col')), may hold values from -6 to 6
- send_rows: int32 [2048, 256], P(('row', 'col')), may hold values from 0 to 2047
- send_count: int32 [2048], P(('row', 'col')), may hold values from 129 to 256, as said below
- hub_rows: int32 [4096], P(('row', 'col')), may hold values from 0 to 2047
- neighbours: int32 [262144, 16], P(('row', 'col')), may hold values from 0 to 10239
- w_self: bfloat16 [256, 256], replicated, may hold values from -0.375 to 0.375
- w_neigh: bfloat16 [256, 256], replicated, may hold values from -0.375 to 0.375
- bias_vector: float32 [256], replicated, may hold values from -3 to 3
- cotangent: bfloat16 [262144, 256], P(('row', 'col')), may hold values from -6 to 6
Outputs:
- output_rows: bfloat16 [262144, 256], P(('row', 'col'))
- feature_grads: float32 [262144, 256], P(('row', 'col'))
Inputs may be any that keep to these rules, and one draw needn't show every extreme that they name: `send_count`: on every device, at least one of its 16 halo lists has its full length 256.
All inputs are finite; a program needn't handle non-finite values.
Results may differ from a plain program's by a relative error of at most 0.003.
Values may be sent and summed in bfloat16 or wider, within the bound.
A program may use at most 128 MiB of HBM per device.

v0:
```python
import math

import jax
import jax.numpy as jnp
from jax import lax
from jax.sharding import PartitionSpec as P


def smooth_gate(values):
    return jax.nn.gelu(values, approximate=True)


def count_matrix(index_rows, column_ids):
    degree = index_rows.shape[1]
    counts = (index_rows[:, 0:1] == column_ids[None, :]).astype(jnp.float32)
    for slot in range(1, degree):
        counts = counts + (index_rows[:, slot : slot + 1] == column_ids[None, :]).astype(
            jnp.float32
        )
    return counts.astype(jnp.bfloat16)


def local(
    features, send_rows, send_count, hub_rows, neighbours, w_self, w_neigh, bias_vector, cotangent
):
    vertex_count, feature_width = features.shape
    slot_count = send_rows.shape[1]
    degree = neighbours.shape[1]
    peer_count = lax.axis_size("col")
    live_mask = jnp.arange(slot_count)[None, :] < send_count[:, None]
    outgoing = jnp.where(live_mask[:, :, None], features[send_rows], jnp.zeros((), features.dtype))
    incoming = lax.all_to_all(outgoing, "col", split_axis=0, concat_axis=0, tiled=True)
    hub_local = features[hub_rows]
    hub_table = lax.all_gather(hub_local, ("row", "col"), axis=0, tiled=True)
    source_table = jnp.concatenate(
        [features, incoming.reshape(-1, feature_width), hub_table], axis=0
    )
    source_count = source_table.shape[0]
    column_ids = jnp.arange(source_count, dtype=jnp.int32)
    block_rows = math.gcd(vertex_count, 512)
    block_count = vertex_count // block_rows
    index_blocks = neighbours.reshape(block_count, block_rows, degree)

    def aggregate(index_rows):
        counts = count_matrix(index_rows, column_ids)
        summed = jnp.dot(counts, source_table, preferred_element_type=jnp.float32)
        return (summed * (1.0 / degree)).astype(jnp.bfloat16)

    aggregated = lax.map(aggregate, index_blocks).reshape(vertex_count, feature_width)
    preact = jnp.dot(features, w_self, preferred_element_type=jnp.float32)
    preact = preact + jnp.dot(aggregated, w_neigh, preferred_element_type=jnp.float32) + bias_vector
    output_rows = smooth_gate(preact).astype(jnp.bfloat16)
    unused, backward = jax.vjp(smooth_gate, preact)
    grad_preact = backward(cotangent.astype(jnp.float32))[0].astype(jnp.bfloat16)
    grad_direct = jnp.dot(grad_preact, w_self.T, preferred_element_type=jnp.float32)
    grad_aggregated = jnp.dot(grad_preact, w_neigh.T, preferred_element_type=jnp.float32).astype(
        jnp.bfloat16
    )
    scaled_grads = (grad_aggregated.astype(jnp.float32) * (1.0 / degree)).astype(jnp.bfloat16)

    def spread(running, inputs):
        index_rows, gradient = inputs
        counts = count_matrix(index_rows, column_ids)
        added = lax.dot_general(
            counts, gradient, (((0,), (0,)), ((), ())), preferred_element_type=jnp.float32
        )
        return (running + added, None)

    table_grads, unused_out = lax.scan(
        spread,
        jnp.zeros((source_count, feature_width), jnp.float32),
        (index_blocks, scaled_grads.reshape(block_count, block_rows, feature_width)),
    )
    hub_start = vertex_count + peer_count * slot_count
    halo_back = table_grads[vertex_count:hub_start].reshape(peer_count, slot_count, feature_width)
    returned = lax.all_to_all(
        halo_back.astype(jnp.bfloat16), "col", split_axis=0, concat_axis=0, tiled=True
    ).astype(halo_back.dtype)
    returned = jnp.where(live_mask[:, :, None], returned, jnp.zeros((), jnp.float32))
    hub_back = table_grads[hub_start:]
    hub_owned = lax.psum_scatter(hub_back, ("row", "col"), scatter_dimension=0, tiled=True)
    grad_rows = grad_direct + table_grads[:vertex_count]
    grad_rows = grad_rows.at[send_rows.reshape(-1)].add(returned.reshape(-1, feature_width))
    grad_rows = grad_rows.at[hub_rows].add(hub_owned)
    return (output_rows, grad_rows)


def solution(mesh):
    return jax.shard_map(
        local,
        mesh=mesh,
        in_specs=(
            P(("row", "col"), None),
            P(("row", "col"), None),
            P(("row", "col")),
            P(("row", "col")),
            P(("row", "col"), None),
            P(),
            P(),
            P(),
            P(("row", "col"), None),
        ),
        out_specs=(P(("row", "col"), None), P(("row", "col"), None)),
        check_vma=False,
    )
```

profile of v0, /device:TPU:0, one launch (start us, length us, event | category | flops | bytes accessed | tf_op | source)
XLA Modules:
  0.0 1190.7 jit_solution(1062293424955180680)
XLA Ops:
  8.4 2.6 gather_fusion.1
  11.8 14.4 %gather_fusion = bf16[4096,256]{1,0:T(8,128)(2,1)S(1)} fusion(bf16[2048,256]{1,0:T(8,128)(2,1)} %param.13, s32[4096]{0:T(1024)S(1)} %broadcast_clamp_fusion), kind=kCustom, calls=%fused_computation | custom fusion | bytes 4210688 | tf_op jit(solution)/shard_map/gather | solution.py:31
  28.0 7.1 all-to-all-start
  38.0 28.2 %all-to-all-done = bf16[16,256,256]{2,1,0:T(8,128)(2,1)S(1)} async-done(((bf16[16,256,256]{2,1,0:T(8,128)(2,1)}), bf16[16,256,256]{2,1,0:T(8,128)(2,1)S(1)}, u32[]{:S(2)}, u32[]{:S(2)}) %all-to-all-start) | async-done | bytes 2097184 | tf_op jit(solution)/shard_map/all_to_all | solution.py:32
  66.2 23.4 %all-gather.3.cloned.1.call-done = bf16[4096,256]{1,0:T(8,128)(2,1)} async-done(((bf16[32,256]{1,0:T(8,128)(2,1)}), bf16[4096,256]{1,0:T(8,128)(2,1)}) %all-gather.3.cloned.1.call-update) | async-done | bytes 2097168 | tf_op jit(solution)/shard_map/all_gather | solution.py:34
  89.6 16.2 %pad_maximum_fusion = bf16[10240,256]{1,0:T(8,128)(2,1)} fusion(bf16[4096,256]{1,0:T(8,128)(2,1)} %all-gather.3.cloned.1.call-done, bf16[4096,256]{1,0:T(8,128)(2,1)S(1)} %bitcast.145, bf16[2048,256]{1,0:T(8,128)(2,1)S(1)} %copy-done.2), kind=kLoop, calls=%fused_computation.67 | loop fusion | flops 15728640 | bytes 10485760 | tf_op jit(solution)/shard_map/concatenate | solution.py:35
  105.8 184.4 %while.24 = (s32[]{:T(128)}, bf16[4,512,256]{2,1,0:T(8,128)(2,1)}, s32[4,512,16]{1,2,0:T(8,128)S(1)}, bf16[10240,256]{1,0:T(8,128)(2,1)}, s32[]{:T(128)}) while((s32[]{:T(128)}, bf16[4,512,256]{2,1,0:T(8,128)(2,1)}, s32[4,512,16]{1,2,0:T(8,128)S(1)}, bf16[10240,256]{1,0:T(8,128)(2,1)}, s32[]{:T(128)}) %tuple.95), condition=%wide.region_1.2_spmd.clone.clone, body=%wide.region_0.1_spmd.clone.clone.sunk | while | flops 2936274944 | bytes 5669441 | solution.py:49
  106.0 46.1 %fusion.62 = bf16[4,512,256]{2,1,0:T(8,128)(2,1)} fusion(bf16[4,512,256]{2,1,0:T(8,128)(2,1)} %get-tuple-element.409, s32[]{:T(128)} %get-tuple-element.408, bf16[10240,256]{1,0:T(8,128)(2,1)} %get-tuple-element.416, s32[512]{0:T(512)S(1)} %bitcast.171, s32[512]{0:T(512)S(1)} %bitcast.172, s32[512]{0:T(512)S(1)} %bitcast.173, s32[512]{0:T(512)S(1)} %bitcast.174, ...), kind=kOutput, calls=%fused_computation.27.clone.1 | convolution fusion | flops 2936274944 | bytes 5538304 | tf_op jit(solution)/shard_map/while/body/eval_jaxpr/dot_general | solution.py:46
  152.2 46.0 %fusion.62 = bf16[4,512,256]{2,1,0:T(8,128)(2,1)} fusion(bf16[4,512,256]{2,1,0:T(8,128)(2,1)} %get-tuple-element.409, s32[]{:T(128)} %get-tuple-element.408, bf16[10240,256]{1,0:T(8,128)(2,1)} %get-tuple-element.416, s32[512]{0:T(512)S(1)} %bitcast.171, s32[512]{0:T(512)S(1)} %bitcast.172, s32[512]{0:T(512)S(1)} %bitcast.173, s32[512]{0:T(512)S(1)} %bitcast.174, ...), kind=kOutput, calls=%fused_computation.27.clone.1 | convolution fusion | flops 2936274944 | bytes 5538304 | tf_op jit(solution)/shard_map/while/body/eval_jaxpr/dot_general | solution.py:46
  198.2 46.0 %fusion.62 = bf16[4,512,256]{2,1,0:T(8,128)(2,1)} fusion(bf16[4,512,256]{2,1,0:T(8,128)(2,1)} %get-tuple-element.409, s32[]{:T(128)} %get-tuple-element.408, bf16[10240,256]{1,0:T(8,128)(2,1)} %get-tuple-element.416, s32[512]{0:T(512)S(1)} %bitcast.171, s32[512]{0:T(512)S(1)} %bitcast.172, s32[512]{0:T(512)S(1)} %bitcast.173, s32[512]{0:T(512)S(1)} %bitcast.174, ...), kind=kOutput, calls=%fused_computation.27.clone.1 | convolution fusion | flops 2936274944 | bytes 5538304 | tf_op jit(solution)/shard_map/while/body/eval_jaxpr/dot_general | solution.py:46
  244.2 46.0 %fusion.62 = bf16[4,512,256]{2,1,0:T(8,128)(2,1)} fusion(bf16[4,512,256]{2,1,0:T(8,128)(2,1)} %get-tuple-element.409, s32[]{:T(128)} %get-tuple-element.408, bf16[10240,256]{1,0:T(8,128)(2,1)} %get-tuple-element.416, s32[512]{0:T(512)S(1)} %bitcast.171, s32[512]{0:T(512)S(1)} %bitcast.172, s32[512]{0:T(512)S(1)} %bitcast.173, s32[512]{0:T(512)S(1)} %bitcast.174, ...), kind=kOutput, calls=%fused_computation.27.clone.1 | convolution fusion | flops 2936274944 | bytes 5538304 | tf_op jit(solution)/shard_map/while/body/eval_jaxpr/dot_general | solution.py:46
  290.2 4.4 fusion.34
  296.1 220.1 %while.25 = (s32[]{:T(128)}, f32[10240,256]{1,0:T(8,128)}, s32[4,512,16]{1,2,0:T(8,128)S(1)}, bf16[4,512,256]{2,1,0:T(8,128)(2,1)S(1)}, s32[]{:T(128)}, /*index=5*/s32[]{:T(128)}) while((s32[]{:T(128)}, f32[10240,256]{1,0:T(8,128)}, s32[4,512,16]{1,2,0:T(8,128)S(1)}, bf16[4,512,256]{2,1,0:T(8,128)(2,1)S(1)}, s32[]{:T(128)}, ...), condition=%wide.region_3.4_spmd.clone.clone, body=%wide.region_2.3_spmd.clone.clone.sunk | while | flops 2941255680 | bytes 21397588 | solution.py:69
  296.4 51.9 %convolution_add_fusion.4 = f32[10240,256]{1,0:T(8,128)} fusion(f32[10240,256]{1,0:T(8,128)} %get-tuple-element.425, s32[512]{0:T(512)S(1)} %bitcast.155, s32[512]{0:T(512)S(1)} %bitcast.156, s32[512]{0:T(512)S(1)} %bitcast.157, s32[512]{0:T(512)S(1)} %bitcast.158, s32[512]{0:T(512)S(1)} %bitcast.159, s32[512]{0:T(512)S(1)} %bitcast.160, ...), kind=kOutput, calls=%fused_computation.46.clone.1 | convolution fusion | flops 2941255680 | bytes 21266436 | tf_op jit(solution)/shard_map/while/body/eval_jaxpr/dot_general | solution.py:64
  348.3 55.9 %convolution_add_fusion.4 = f32[10240,256]{1,0:T(8,128)} fusion(f32[10240,256]{1,0:T(8,128)} %get-tuple-element.425, s32[512]{0:T(512)S(1)} %bitcast.155, s32[512]{0:T(512)S(1)} %bitcast.156, s32[512]{0:T(512)S(1)} %bitcast.157, s32[512]{0:T(512)S(1)} %bitcast.158, s32[512]{0:T(512)S(1)} %bitcast.159, s32[512]{0:T(512)S(1)} %bitcast.160, ...), kind=kOutput, calls=%fused_computation.46.clone.1 | convolution fusion | flops 2941255680 | bytes 21266436 | tf_op jit(solution)/shard_map/while/body/eval_jaxpr/dot_general | solution.py:64
  404.2 55.9 %convolution_add_fusion.4 = f32[10240,256]{1,0:T(8,128)} fusion(f32[10240,256]{1,0:T(8,128)} %get-tuple-element.425, s32[512]{0:T(512)S(1)} %bitcast.155, s32[512]{0:T(512)S(1)} %bitcast.156, s32[512]{0:T(512)S(1)} %bitcast.157, s32[512]{0:T(512)S(1)} %bitcast.158, s32[512]{0:T(512)S(1)} %bitcast.159, s32[512]{0:T(512)S(1)} %bitcast.160, ...), kind=kOutput, calls=%fused_computation.46.clone.1 | convolution fusion | flops 2941255680 | bytes 21266436 | tf_op jit(solution)/shard_map/while/body/eval_jaxpr/dot_general | solution.py:64
  460.1 55.9 %convolution_add_fusion.4 = f32[10240,256]{1,0:T(8,128)} fusion(f32[10240,256]{1,0:T(8,128)} %get-tuple-element.425, s32[512]{0:T(512)S(1)} %bitcast.155, s32[512]{0:T(512)S(1)} %bitcast.156, s32[512]{0:T(512)S(1)} %bitcast.157, s32[512]{0:T(512)S(1)} %bitcast.158, s32[512]{0:T(512)S(1)} %bitcast.159, s32[512]{0:T(512)S(1)} %bitcast.160, ...), kind=kOutput, calls=%fused_computation.46.clone.1 | convolution fusion | flops 2941255680 | bytes 21266436 | tf_op jit(solution)/shard_map/while/body/eval_jaxpr/dot_general | solution.py:64
  516.2 4.6 slice.108
  520.9 3.7 slice.212
  524.6 4.7 all-to-all-start.1
  531.4 28.7 %all-to-all-done.1 = bf16[16,256,256]{2,1,0:T(8,128)(2,1)} async-done(((bf16[16,256,256]{2,1,0:T(8,128)(2,1)}), bf16[16,256,256]{2,1,0:T(8,128)(2,1)}, u32[]{:S(2)}, u32[]{:S(2)}) %all-to-all-start.1) | async-done | bytes 2097184 | tf_op jit(solution)/shard_map/all_to_all | solution.py:76
  560.1 3.5 convert_select_fusion
  563.6 23.6 %scatter_fusion = f32[2048,256]{1,0:T(8,128)S(1)} fusion(f32[2048,256]{1,0:T(8,128)S(1)} %convolution_add_fusion.1, s32[4096]{0:T(1024)S(1)} %bitcast.150, f32[4096,256]{1,0:T(8,128)} %bitcast.144), kind=kCustom, calls=%fused_computation.2 | custom fusion | flops 1048576 | bytes 12599296 | tf_op jit(solution)/shard_map/scatter-add | solution.py:83
  587.2 593.1 %reduce-scatter.2.cloned.1.call-done = f32[32,256]{1,0:T(8,128)} async-done(((f32[4096,256]{1,0:T(8,128)}), f32[32,256]{1,0:T(8,128)}) %reduce-scatter.2.cloned.1.call-update) | async-done | bytes 32784 | tf_op jit(solution)/shard_map/reduce_scatter | solution.py:81
  (66 shorter events, 13.4 us)
Async XLA Ops:
  7.2 283.0 %copy-start = (bf16[256,256]{1,0:T(8,128)(2,1)S(1)}, bf16[256,256]{1,0:T(8,128)(2,1)}, u32[]{:S(2)}) copy-start(bf16[256,256]{1,0:T(8,128)(2,1)} %param.19) | copy-start | bytes 393220
  7.2 19.1 %copy-start.13 = (s32[16]{0:T(128)S(1)}, s32[16]{0:T(128)}, u32[]{:S(2)}) copy-start(s32[16]{0:T(128)} %param.15) | copy-start | bytes 196
  7.2 82.4 %all-gather.3.cloned.1.call-start = ((), (), s32[]{:S(2)}) async-start(), calls=%async_computation.4 | async-start | bytes 2113536 | tf_op jit(solution)/shard_map/all_gather | solution.py:34
  7.9 0.5 copy-start.11
  11.8 24.4 %copy-start.2 = (bf16[2048,256]{1,0:T(8,128)(2,1)S(1)}, bf16[2048,256]{1,0:T(8,128)(2,1)}, u32[]{:S(2)}) copy-start(bf16[2048,256]{1,0:T(8,128)(2,1)} %param.13) | copy-start | bytes 3145732
  11.8 24.4 %copy-start.6 = (bf16[256,256]{1,0:T(8,128)(2,1)S(1)}, bf16[256,256]{1,0:T(8,128)(2,1)}, u32[]{:S(2)}) copy-start(bf16[256,256]{1,0:T(8,128)(2,1)} %param.18) | copy-start | bytes 393220
  26.3 8.9 copy-start.9
  28.0 38.1 %all-to-all-start = ((bf16[16,256,256]{2,1,0:T(8,128)(2,1)}), bf16[16,256,256]{2,1,0:T(8,128)(2,1)S(1)}, u32[]{:S(2)}, u32[]{:S(2)}) async-start(bf16[16,256,256]{2,1,0:T(8,128)(2,1)} %broadcast_select_fusion), calls=%async_computation | async-start | bytes 4194304 | tf_op jit(solution)/shard_map/all_to_all | solution.py:32
  35.2 1145.1 %reduce-scatter.2.cloned.1.call-start = ((), (), s32[]{:S(2)}) async-start(), calls=%async_computation.3 | async-start | bytes 4227072 | tf_op jit(solution)/shard_map/reduce_scatter | solution.py:81
  105.8 184.4 %copy-start.5 = (f32[2048,256]{1,0:T(8,128)S(1)}, f32[2048,256]{1,0:T(8,128)}, u32[]{:S(2)}) copy-start(f32[2048,256]{1,0:T(8,128)} %fusion.45) | copy-start | bytes 6291460
  105.8 184.4 %copy-start.14 = (f32[256]{0:T(256)S(1)}, f32[256]{0:T(256)}, u32[]{:S(2)}) copy-start(f32[256]{0:T(256)} %param.20) | copy-start | bytes 3076
  294.6 1.0 copy-start.3
  516.2 13.1 %copy-start.8 = (s32[16,256]{1,0:T(8,128)S(1)}, s32[16,256]{1,0:T(8,128)}, u32[]{:S(2)}) copy-start(s32[16,256]{1,0:T(8,128)} %param.14) | copy-start | bytes 49156
  516.2 13.1 %copy-start.4 = (bf16[2048,256]{1,0:T(8,128)(2,1)S(1)}, bf16[2048,256]{1,0:T(8,128)(2,1)}, u32[]{:S(2)}) copy-start(bf16[2048,256]{1,0:T(8,128)(2,1)} %copy-done.3) | copy-start | bytes 3145732
  516.2 13.1 %copy-start.7 = (bf16[256,256]{1,0:T(8,128)(2,1)S(1)}, bf16[256,256]{1,0:T(8,128)(2,1)}, u32[]{:S(2)}) copy-start(bf16[256,256]{1,0:T(8,128)(2,1)} %param.18) | copy-start | bytes 393220
  520.8 39.2 %copy-start.10 = (pred[16,256]{1,0:T(8,128)(4,1)S(1)}, pred[16,256]{1,0:T(8,128)(4,1)}, u32[]{:S(2)}) copy-start(pred[16,256]{1,0:T(8,128)(4,1)} %copy-done.9) | copy-start | bytes 12292
  524.6 35.5 %all-to-all-start.1 = ((bf16[16,256,256]{2,1,0:T(8,128)(2,1)}), bf16[16,256,256]{2,1,0:T(8,128)(2,1)}, u32[]{:S(2)}, u32[]{:S(2)}) async-start(bf16[16,256,256]{2,1,0:T(8,128)(2,1)} %bitcast.5), calls=%async_computation.1 | async-start | bytes 4194304 | tf_op jit(solution)/shard_map/all_to_all | solution.py:76
  563.6 616.7 %copy-start.12 = (s32[32]{0:T(128)S(1)}, s32[32]{0:T(128)}, u32[]{:S(2)}) copy-start(s32[32]{0:T(128)} %copy-done.11) | copy-start | bytes 388
  1182.1 1.3 copy-start.1
Sparse Core Ops, SparseCore 0:
  11.6 78.0 all-gather.2
  521.0 659.2 reduce-scatter.1
where the time goes:
time: 1200 us; the launch traced here: 1190 us
  waiting for transfers between devices  673 us (56%)
  matrix products  412 us (34%)
  other arithmetic  48.2 us (4%)
  local copies, waits for them, and re-layouts  29.4 us (2%)
  between operations  14.7 us (1%)
    reduce_scatter x1, waiting for transfers between devices, local(): lax.psum_scatter(hub_back, ('row', 'col'), scatter_dimension=0, tiled=True)  593 us
    dot_general x4, matrix products, spread(): lax.dot_general(counts, gradient, (((0,), (0,)), ((), ())), preferred_ele...  219 us
    dot_general x4, matrix products, aggregate(): summed = jnp.dot(counts, source_table, preferred_element_type=jnp.float32)  184 us
    all_to_all x1, waiting for transfers between devices, local(): lax.all_to_all(halo_back.astype(jnp.bfloat16), 'col', split_axis=0, conca...  28.7 us
    all_to_all x1, waiting for transfers between devices, local(): lax.all_to_all(outgoing, 'col', split_axis=0, concat_axis=0, tiled=True)  28.2 us
  transfers between devices with their start and end apart: 4, of which 4 were waited for; matrix products, arithmetic and copies ran while one was open for 4% of the time, Pallas kernels for 0%

commit v1 on v0

v1 whole, which is shorter than its diff:
```python
import jax
import jax.numpy as jnp
from jax import lax
from jax.sharding import PartitionSpec as P


def smooth_gate(values):
    return jax.nn.gelu(values, approximate=True)


def count_matrix(index_rows, start, width):
    degree = index_rows.shape[1]
    column_ids = jnp.arange(start, start + width, dtype=jnp.int32)
    counts = (index_rows[:, 0:1] == column_ids[None, :]).astype(jnp.float32)
    for slot in range(1, degree):
        counts = counts + (index_rows[:, slot : slot + 1] == column_ids[None, :]).astype(
            jnp.float32
        )
    return counts.astype(jnp.bfloat16)


def transposed_dot(counts, values):
    return lax.dot_general(
        counts, values, (((0,), (0,)), ((), ())), preferred_element_type=jnp.float32
    )


def local(
    features, send_rows, send_count, hub_rows, neighbours, w_self, w_neigh, bias_vector, cotangent
):
    vertex_count, feature_width = features.shape
    slot_count = send_rows.shape[1]
    degree = neighbours.shape[1]
    peer_count = lax.axis_size("col")
    hub_count = hub_rows.shape[0]
    device_count = lax.axis_size("row") * peer_count
    halo_width = peer_count * slot_count
    hub_start = vertex_count + halo_width
    live_mask = jnp.arange(slot_count)[None, :] < send_count[:, None]
    outgoing = jnp.where(live_mask[:, :, None], features[send_rows], jnp.zeros((), features.dtype))
    incoming = lax.all_to_all(outgoing, "col", split_axis=0, concat_axis=0, tiled=True)
    incoming = incoming.reshape(-1, feature_width)
    hub_local = features[hub_rows]
    hub_table = lax.all_gather(hub_local, ("row", "col"), axis=0, tiled=True)

    counts_own = count_matrix(neighbours, 0, vertex_count)
    counts_halo = count_matrix(neighbours, vertex_count, halo_width)
    counts_hub = count_matrix(neighbours, hub_start, device_count * hub_count)
    counts_own, counts_halo, counts_hub = lax.optimization_barrier(
        (counts_own, counts_halo, counts_hub)
    )

    summed = jnp.dot(counts_own, features, preferred_element_type=jnp.float32)
    summed = summed + jnp.dot(counts_halo, incoming, preferred_element_type=jnp.float32)
    summed = summed + jnp.dot(counts_hub, hub_table, preferred_element_type=jnp.float32)
    aggregated = (summed * (1.0 / degree)).astype(jnp.bfloat16)
    preact = jnp.dot(features, w_self, preferred_element_type=jnp.float32)
    preact = preact + jnp.dot(aggregated, w_neigh, preferred_element_type=jnp.float32) + bias_vector
    output_rows = smooth_gate(preact).astype(jnp.bfloat16)
    unused, backward = jax.vjp(smooth_gate, preact)
    grad_preact = backward(cotangent.astype(jnp.float32))[0].astype(jnp.bfloat16)
    grad_direct = jnp.dot(grad_preact, w_self.T, preferred_element_type=jnp.float32)
    grad_aggregated = jnp.dot(grad_preact, w_neigh.T, preferred_element_type=jnp.float32).astype(
        jnp.bfloat16
    )
    scaled_grads = (grad_aggregated.astype(jnp.float32) * (1.0 / degree)).astype(jnp.bfloat16)

    hub_back = transposed_dot(counts_hub, scaled_grads)
    hub_parts = lax.all_to_all(
        hub_back.reshape(device_count, hub_count, feature_width),
        ("row", "col"),
        split_axis=0,
        concat_axis=0,
        tiled=True,
    )
    hub_owned = jnp.sum(hub_parts, axis=0)

    halo_back = transposed_dot(counts_halo, scaled_grads)
    returned = lax.all_to_all(
        halo_back.astype(jnp.bfloat16).reshape(peer_count, slot_count, feature_width),
        "col",
        split_axis=0,
        concat_axis=0,
        tiled=True,
    ).astype(jnp.float32)
    returned = jnp.where(live_mask[:, :, None], returned, jnp.zeros((), jnp.float32))
    grad_rows = grad_direct + transposed_dot(counts_own, scaled_grads)
    grad_rows = grad_rows.at[send_rows.reshape(-1)].add(returned.reshape(-1, feature_width))
    grad_rows = grad_rows.at[hub_rows].add(hub_owned)
    return (output_rows, grad_rows)


def solution(mesh):
    return jax.shard_map(
        local,
        mesh=mesh,
        in_specs=(
            P(("row", "col"), None),
            P(("row", "col"), None),
            P(("row", "col")),
            P(("row", "col")),
            P(("row", "col"), None),
            P(),
            P(),
            P(),
            P(("row", "col"), None),
        ),
        out_specs=(P(("row", "col"), None), P(("row", "col"), None)),
        check_vma=False,
    )
```

time: 1200 us -> 337 us (0.28)
  waiting for transfers between devices: 673 us -> 36.1 us
  matrix products: 412 us -> 62 us
  other arithmetic: 48.2 us -> 182 us
  local copies, waits for them, and re-layouts: 29.4 us -> 17.3 us
    reduce_scatter x1 -> x0, waiting for transfers between devices: 593 us -> none  [local(): lax.psum_scatter(hub_back, ('row', 'col'), scatter_dimension=0, tiled=True)]
    dot_general x8 -> x5, matrix products: 404 us -> 48.5 us  [the longest x3 26.6 us: transposed_dot(): lax.dot_general(counts, values, (((0,), (0,)), ((), ())), preferred_eleme...]
    convert_element_type x0 -> x2, other arithmetic: none -> 148 us  [count_matrix(): return counts.astype(jnp.bfloat16)]
    all_to_all x1, waiting for transfers between devices: 28.2 us -> 0.01 us  [local(): lax.all_to_all(outgoing, 'col', split_axis=0, concat_axis=0, tiled=True)]
    all_gather x1, waiting for transfers between devices: 23.4 us -> 0.01 us  [local(): hub_table = lax.all_gather(hub_local, ('row', 'col'), axis=0, tiled=True)]
    concatenate x1 -> x0, other arithmetic: 16.2 us -> none  [local(): jnp.concatenate([features, incoming.reshape(-1, feature_width), hub_table...]
    all_to_all x1 -> x2, waiting for transfers between devices: 28.7 us -> 36.1 us  [the longest x1 19 us: local(): lax.all_to_all(halo_back.astype(jnp.bfloat16).reshape(peer_count, slot_co...]
  transfers between devices with their start and end apart: 4 -> 4, of which waited for: 4 -> 2; matrix products, arithmetic and copies ran while one was open for 4% -> 61% of each run, Pallas kernels for 0% -> 0%
where the time goes in v1:
time: 337 us; the launch traced here: 335 us
  other arithmetic  182 us (54%)
  matrix products  62 us (18%)
  waiting for transfers between devices  36.1 us (11%)
  starting transfers between devices  22.9 us (7%)
  local copies, waits for them, and re-layouts  17.3 us (5%)
  between operations  14.3 us (4%)
    convert_element_type x2, other arithmetic, count_matrix(): return counts.astype(jnp.bfloat16)  148 us
    dot_general x3, matrix products, transposed_dot(): lax.dot_general(counts, values, (((0,), (0,)), ((), ())), preferred_eleme...  26.6 us
    scatter-add x1, other arithmetic, local(): grad_rows.at[send_rows.reshape(-1)].add(returned.reshape(-1, feature_width))  23.6 us
    all_to_all x1, waiting for transfers between devices, local(): lax.all_to_all(halo_back.astype(jnp.bfloat16).reshape(peer_count, slot_co...  19 us
    all_to_all x1, waiting for transfers between devices, local(): lax.all_to_all(hub_back.reshape(device_count, hub_count, feature_width),...  17.1 us
    gather x1, local copies, waits for them, and re-layouts, local(): features[send_rows]  14.6 us
    dot_general x1, matrix products, local(): jnp.dot(counts_hub, hub_table, preferred_element_type=jnp.float32)  12.4 us
    dot_general x1, matrix products, local(): jnp.dot(aggregated, w_neigh, preferred_element_type=jnp.float32)  10.8 us
  transfers between devices with their start and end apart: 4, of which 2 were waited for; matrix products, arithmetic and copies ran while one was open for 61% of the time, Pallas kernels for 0%

profile of v1, /device:TPU:0, one launch (start us, length us, event | category | flops | bytes accessed | tf_op | source)
XLA Modules:
  0.0 335.0 jit_solution(12844590273658027493)
XLA Ops:
  7.2 0.8 iota_compare_fusion.16
  8.0 0.7 fusion.18
  8.8 14.6 %gather_fusion = bf16[4096,256]{1,0:T(8,128)(2,1)S(1)} fusion(bf16[2048,256]{1,0:T(8,128)(2,1)S(1)} %copy-done, s32[4096]{0:T(1024)S(1)} %broadcast_clamp_fusion), kind=kCustom, calls=%fused_computation | custom fusion | bytes 4210688 | tf_op jit(solution)/shard_map/gather | solution.py:40
  23.4 1.7 broadcast_select_fusion
  25.1 7.1 %all-to-all-start = ((bf16[16,256,256]{2,1,0:T(8,128)(2,1)}), bf16[16,256,256]{2,1,0:T(8,128)(2,1)S(1)}, u32[]{:S(2)}, u32[]{:S(2)}) async-start(bf16[16,256,256]{2,1,0:T(8,128)(2,1)} %broadcast_select_fusion), calls=%async_computation | async-start | bytes 4194304 | tf_op jit(solution)/shard_map/all_to_all | solution.py:41
  32.3 1.2 gather_fusion.1
  33.7 107.5 %add_convert_fusion = (bf16[2048,4096]{1,0:T(8,128)(2,1)}, bf16[2048,4096]{1,0:T(8,128)(2,1)}) fusion(s32[4096]{0:T(1024)S(1)} %get-tuple-element.28, s32[2048]{0:T(1024)S(1)} %bitcast.81, s32[2048]{0:T(1024)S(1)} %bitcast.83, s32[2048]{0:T(1024)S(1)} %bitcast.55, s32[2048]{0:T(1024)S(1)} %bitcast.57, s32[2048]{0:T(1024)S(1)} %bitcast.59, ...), kind=kLoop, calls=%fused_computation.4 | loop fusion | flops 805306368 | bytes 33718272 | tf_op jit(solution)/shard_map/convert_element_type | solution.py:19
  141.3 40.4 %add_convert_fusion.2 = bf16[2048,2048]{1,0:T(8,128)(2,1)} fusion(s32[2048]{0:T(1024)S(1)} %bitcast.82, s32[2048]{0:T(1024)S(1)} %bitcast.84, s32[2048]{0:T(1024)S(1)} %bitcast.56, s32[2048]{0:T(1024)S(1)} %bitcast.58, s32[2048]{0:T(1024)S(1)} %bitcast.60, s32[2048]{0:T(1024)S(1)} %bitcast.62, s32[2048]{0:T(1024)S(1)} %bitcast.64, s32[2048]{0:T(1024)S(1)} %bitcast.66, ...), kind=kLoop, calls=%fused_computation.6 | loop fusion | flops 201326592 | bytes 8519680 | tf_op jit(solution)/shard_map/convert_element_type | solution.py:19
  181.6 1.7 fusion.21
  183.4 9.5 %fusion.22 = f32[2048,256]{1,0:T(8,128)} fusion(bf16[2048,4096]{1,0:T(8,128)(2,1)} %get-tuple-element.6, bf16[4096,256]{1,0:T(8,128)(2,1)S(1)} %bitcast.51), kind=kOutput, calls=%fused_computation.65 | convolution fusion | flops 4294967296 | bytes 20971520 | tf_op jit(solution)/shard_map/dot_general | solution.py:54
  192.9 12.4 %fusion.23 = f32[2048,256]{1,0:T(8,128)} fusion(bf16[2048,4096]{1,0:T(8,128)(2,1)} %get-tuple-element.7, bf16[4096,256]{1,0:T(8,128)(2,1)} %all-gather.3.cloned.1.call-done), kind=kOutput, calls=%fused_computation.66 | convolution fusion | flops 4294967296 | bytes 20971520 | tf_op jit(solution)/shard_map/dot_general | solution.py:55
  205.3 10.8 %fusion.9 = (bf16[2048,256]{1,0:T(8,128)(2,1)S(1)}, bf16[2048,256]{1,0:T(8,128)(2,1)}) fusion(bf16[2048,256]{1,0:T(8,128)(2,1)} %param.17, f32[256]{0:T(256)S(1)} %copy-done.11, f32[2048,256]{1,0:T(8,128)} %fusion.21, bf16[256,256]{1,0:T(8,128)(2,1)S(1)} %copy-done.8, f32[2048,256]{1,0:T(8,128)} %fusion.23, f32[2048,256]{1,0:T(8,128)} %fusion.22, ...), kind=kOutput, calls=%fused_computation.42 | convolution fusion | flops 2431123456 | bytes 19006464 | tf_op jit(solution)/shard_map/dot_general | solution.py:58
  216.5 10.2 %convolution_convert_fusion = bf16[4096,256]{1,0:T(8,128)(2,1)} fusion(bf16[2048,4096]{1,0:T(8,128)(2,1)} %get-tuple-element.6, bf16[2048,256]{1,0:T(8,128)(2,1)S(1)} %fusion.6), kind=kOutput, calls=%fused_computation.23 | convolution fusion | flops 4296015872 | bytes 19922944 | tf_op jit(solution)/shard_map/dot_general | solution.py:23
  226.7 7.2 %all-to-all-start.1 = ((bf16[16,256,256]{2,1,0:T(8,128)(2,1)}), bf16[16,256,256]{2,1,0:T(8,128)(2,1)S(1)}, u32[]{:S(2)}, u32[]{:S(2)}) async-start(bf16[16,256,256]{2,1,0:T(8,128)(2,1)} %bitcast.52), calls=%async_computation.1 | async-start | bytes 4194304 | tf_op jit(solution)/shard_map/all_to_all | solution.py:79
  234.0 10.2 %fusion.25 = f32[4096,256]{1,0:T(8,128)} fusion(bf16[2048,4096]{1,0:T(8,128)(2,1)} %get-tuple-element.7, bf16[2048,256]{1,0:T(8,128)(2,1)S(1)} %fusion.6), kind=kOutput, calls=%fused_computation.68 | convolution fusion | flops 4294967296 | bytes 22020096 | tf_op jit(solution)/shard_map/dot_general | solution.py:23
  244.2 19.0 %all-to-all-done.1 = bf16[16,256,256]{2,1,0:T(8,128)(2,1)S(1)} async-done(((bf16[16,256,256]{2,1,0:T(8,128)(2,1)}), bf16[16,256,256]{2,1,0:T(8,128)(2,1)S(1)}, u32[]{:S(2)}, u32[]{:S(2)}) %all-to-all-start.1) | async-done | bytes 2097184 | tf_op jit(solution)/shard_map/all_to_all | solution.py:79
  263.2 8.5 %all-to-all-start.2 = ((f32[128,32,256]{2,1,0:T(8,128)}), f32[128,32,256]{2,1,0:T(8,128)}, u32[]{:S(2)}, u32[]{:S(2)}) async-start(f32[128,32,256]{2,1,0:T(8,128)} %bitcast.50), calls=%async_computation.2 | async-start | bytes 8388608 | tf_op jit(solution)/shard_map/all_to_all | solution.py:69
  271.9 6.2 %fusion.24 = f32[2048,256]{1,0:T(8,128)S(1)} fusion(bf16[2048,2048]{1,0:T(8,128)(2,1)} %add_convert_fusion.2, bf16[2048,256]{1,0:T(8,128)(2,1)} %copy-done.6), kind=kOutput, calls=%fused_computation.67 | convolution fusion | flops 2147483648 | bytes 11534336 | tf_op jit(solution)/shard_map/dot_general | solution.py:23
  278.6 3.5 %convert_select_fusion = f32[16,256,256]{2,1,0:T(8,128)} fusion(bf16[16,256,256]{2,1,0:T(8,128)(2,1)} %copy-done.3, pred[16,256]{1,0:T(8,128)(4,1)S(1)} %iota_compare_fusion.16), kind=kLoop, calls=%fused_computation.24 | loop fusion | flops 2097152 | bytes 6295552 | tf_op jit(solution)/shard_map/jit(_where)/select_n | solution.py:86
  282.1 23.6 %scatter_fusion = f32[2048,256]{1,0:T(8,128)S(1)} fusion(f32[2048,256]{1,0:T(8,128)S(1)} %convolution_add_fusion, s32[4096]{0:T(1024)S(1)} %bitcast.85, f32[4096,256]{1,0:T(8,128)} %bitcast.48), kind=kCustom, calls=%fused_computation.2 | custom fusion | flops 1048576 | bytes 12599296 | tf_op jit(solution)/shard_map/scatter-add | solution.py:88
  305.7 17.1 %all-to-all-done.2 = f32[128,32,256]{2,1,0:T(8,128)} async-done(((f32[128,32,256]{2,1,0:T(8,128)}), f32[128,32,256]{2,1,0:T(8,128)}, u32[]{:S(2)}, u32[]{:S(2)}) %all-to-all-start.2) | async-done | bytes 4194336 | tf_op jit(solution)/shard_map/all_to_all | solution.py:69
  322.8 2.5 reduce_sum.9
  325.3 1.5 scatter_fusion.1
  326.8 1.3 copy-done.2
  (39 shorter events, 1.2 us)
Async XLA Ops:
  7.2 1.6 copy-start
  7.2 25.1 %copy-start.12 = (s32[32]{0:T(128)S(1)}, s32[32]{0:T(128)}, u32[]{:S(2)}) copy-start(s32[32]{0:T(128)} %param.12) | copy-start | bytes 388
  7.2 26.4 %copy-start.9 = (s32[2048,16]{0,1:T(8,128)S(1)}, s32[2048,16]{0,1:T(8,128)}, u32[]{:S(2)}) copy-start(s32[2048,16]{0,1:T(8,128)} %param.13) | copy-start | bytes 393220
  25.1 158.3 %all-to-all-start = ((bf16[16,256,256]{2,1,0:T(8,128)(2,1)}), bf16[16,256,256]{2,1,0:T(8,128)(2,1)S(1)}, u32[]{:S(2)}, u32[]{:S(2)}) async-start(bf16[16,256,256]{2,1,0:T(8,128)(2,1)} %broadcast_select_fusion), calls=%async_computation | async-start | bytes 4194304 | tf_op jit(solution)/shard_map/all_to_all | solution.py:41
  32.2 160.6 %all-gather.3.cloned.1.call-start = ((), (), s32[]{:S(2)}) async-start(), calls=%async_computation.3 | async-start | bytes 2113536 | tf_op jit(solution)/shard_map/all_gather | solution.py:44
  33.7 147.9 %copy-start.7 = (bf16[256,256]{1,0:T(8,128)(2,1)S(1)}, bf16[256,256]{1,0:T(8,128)(2,1)}, u32[]{:S(2)}) copy-start(bf16[256,256]{1,0:T(8,128)(2,1)} %param.14) | copy-start | bytes 393220
  192.9 12.4 %copy-start.8 = (bf16[256,256]{1,0:T(8,128)(2,1)S(1)}, bf16[256,256]{1,0:T(8,128)(2,1)}, u32[]{:S(2)}) copy-start(bf16[256,256]{1,0:T(8,128)(2,1)} %param.15) | copy-start | bytes 393220
  192.9 12.4 %copy-start.11 = (f32[256]{0:T(256)S(1)}, f32[256]{0:T(256)}, u32[]{:S(2)}) copy-start(f32[256]{0:T(256)} %param.16) | copy-start | bytes 3076
  216.1 10.7 %copy-start.4 = (bf16[2048,256]{1,0:T(8,128)(2,1)}, bf16[2048,256]{1,0:T(8,128)(2,1)S(1)}, u32[]{:S(2)}) copy-start(bf16[2048,256]{1,0:T(8,128)(2,1)S(1)} %get-tuple-element.8) | copy-start | bytes 3145732
  216.5 17.4 %copy-start.6 = (bf16[2048,256]{1,0:T(8,128)(2,1)}, bf16[2048,256]{1,0:T(8,128)(2,1)S(1)}, u32[]{:S(2)}) copy-start(bf16[2048,256]{1,0:T(8,128)(2,1)S(1)} %fusion.6) | copy-start | bytes 3145732
  226.7 36.5 %all-to-all-start.1 = ((bf16[16,256,256]{2,1,0:T(8,128)(2,1)}), bf16[16,256,256]{2,1,0:T(8,128)(2,1)S(1)}, u32[]{:S(2)}, u32[]{:S(2)}) async-start(bf16[16,256,256]{2,1,0:T(8,128)(2,1)} %bitcast.52), calls=%async_computation.1 | async-start | bytes 4194304 | tf_op jit(solution)/shard_map/all_to_all | solution.py:79
  234.0 37.8 %copy-start.10 = (s32[16,256]{1,0:T(8,128)S(1)}, s32[16,256]{1,0:T(8,128)}, u32[]{:S(2)}) copy-start(s32[16,256]{1,0:T(8,128)} %param.10) | copy-start | bytes 49156
  244.2 33.9 %copy-start.5 = (bf16[2048,256]{1,0:T(8,128)(2,1)S(1)}, bf16[2048,256]{1,0:T(8,128)(2,1)}, u32[]{:S(2)}) copy-start(bf16[2048,256]{1,0:T(8,128)(2,1)} %copy-done.4) | copy-start | bytes 3145732
  263.2 8.6 %copy-start.3 = (bf16[16,256,256]{2,1,0:T(8,128)(2,1)}, bf16[16,256,256]{2,1,0:T(8,128)(2,1)S(1)}, u32[]{:S(2)}) copy-start(bf16[16,256,256]{2,1,0:T(8,128)(2,1)S(1)} %all-to-all-done.1) | copy-start | bytes 6291460
  263.2 59.6 %all-to-all-start.2 = ((f32[128,32,256]{2,1,0:T(8,128)}), f32[128,32,256]{2,1,0:T(8,128)}, u32[]{:S(2)}, u32[]{:S(2)}) async-start(f32[128,32,256]{2,1,0:T(8,128)} %bitcast.50), calls=%async_computation.2 | async-start | bytes 8388608 | tf_op jit(solution)/shard_map/all_to_all | solution.py:69
  282.1 46.0 %copy-start.1 = (bf16[2048,256]{1,0:T(8,128)(2,1)S(1)}, bf16[2048,256]{1,0:T(8,128)(2,1)}, u32[]{:S(2)}) copy-start(bf16[2048,256]{1,0:T(8,128)(2,1)} %param.9) | copy-start | bytes 3145732
  326.8 1.3 copy-start.2
Sparse Core Ops, SparseCore 0:
  36.6 72.8 all-gather.2

commit v2 on v1

--- a/solution.py
+++ b/solution.py
@@ -37,7 +37,11 @@
     halo_width = peer_count * slot_count
     hub_start = vertex_count + halo_width
     live_mask = jnp.arange(slot_count)[None, :] < send_count[:, None]
-    outgoing = jnp.where(live_mask[:, :, None], features[send_rows], jnp.zeros((), features.dtype))
+    row_ids = jnp.arange(vertex_count, dtype=jnp.int32)
+    picks = ((send_rows[:, :, None] == row_ids) & live_mask[:, :, None]).astype(features.dtype)
+    picks = picks.reshape(halo_width, vertex_count)
+    outgoing = jnp.dot(picks, features, preferred_element_type=jnp.float32).astype(features.dtype)
+    outgoing = outgoing.reshape(peer_count, slot_count, feature_width)
     incoming = lax.all_to_all(outgoing, "col", split_axis=0, concat_axis=0, tiled=True)
     incoming = incoming.reshape(-1, feature_width)
     hub_local = features[hub_rows]
@@ -82,10 +86,9 @@
         split_axis=0,
         concat_axis=0,
         tiled=True,
-    ).astype(jnp.float32)
-    returned = jnp.where(live_mask[:, :, None], returned, jnp.zeros((), jnp.float32))
+    )
     grad_rows = grad_direct + transposed_dot(counts_own, scaled_grads)
-    grad_rows = grad_rows.at[send_rows.reshape(-1)].add(returned.reshape(-1, feature_width))
+    grad_rows = grad_rows + transposed_dot(picks, returned.reshape(halo_width, feature_width))
     grad_rows = grad_rows.at[hub_rows].add(hub_owned)
     return (output_rows, grad_rows)
 

time: 337 us -> 331 us (0.982)
  other arithmetic: 182 us -> 153 us
  waiting for transfers between devices: 36.1 us -> 55.1 us
  matrix products: 62 us -> 79.2 us
  local copies, waits for them, and re-layouts: 17.3 us -> 3.86 us
    scatter-add x1 -> x0, other arithmetic: 23.6 us -> none  [local(): grad_rows.at[send_rows.reshape(-1)].add(returned.reshape(-1, feature_width))]
    all_to_all x1, waiting for transfers between devices: 17.1 us -> 35.9 us  [local(): lax.all_to_all(hub_back.reshape(device_count, hub_count, feature_width),...]
    gather x1 -> x0, local copies, waits for them, and re-layouts: 14.6 us -> none  [local(): features[send_rows]]
    dot_general x0 -> x1, matrix products: none -> 9.18 us  [local(): jnp.dot(picks, features, preferred_element_type=jnp.float32)]
    dot_general x3 -> x4, matrix products: 26.6 us -> 34.7 us  [transposed_dot(): lax.dot_general(counts, values, (((0,), (0,)), ((), ())), preferred_eleme...]
    select_n x3 -> x0, other arithmetic: 5.23 us -> none  [the longest x1 3.54 us: local(): jnp.where(live_mask[:, :, None], returned, jnp.zeros((), jnp.float32))]
  transfers between devices with their start and end apart: 4 -> 4, of which waited for: 2 -> 2; matrix products, arithmetic and copies ran while one was open for 61% -> 59% of each run, Pallas kernels for 0% -> 0%
where the time goes in v2:
time: 331 us; the launch traced here: 329 us
  other arithmetic  153 us (46%)
  matrix products  79.2 us (24%)
  waiting for transfers between devices  55.1 us (17%)
  starting transfers between devices  22.9 us (7%)
  between operations  14.2 us (4%)
  local copies, waits for them, and re-layouts  3.86 us (1%)
    convert_element_type x2, other arithmetic, count_matrix(): return counts.astype(jnp.bfloat16)  148 us
    all_to_all x1, waiting for transfers between devices, local(): lax.all_to_all(hub_back.reshape(device_count, hub_count, feature_width),...  35.9 us
    dot_general x4, matrix products, transposed_dot(): lax.dot_general(counts, values, (((0,), (0,)), ((), ())), preferred_eleme...  34.7 us
    all_to_all x1, waiting for transfers between devices, local(): lax.all_to_all(halo_back.astype(jnp.bfloat16).reshape(peer_count, slot_co...  19.2 us
    dot_general x1, matrix products, local(): jnp.dot(counts_hub, hub_table, preferred_element_type=jnp.float32)  12.4 us
    dot_general x1, matrix products, local(): jnp.dot(aggregated, w_neigh, preferred_element_type=jnp.float32)  10.8 us
    dot_general x1, matrix products, local(): jnp.dot(counts_halo, incoming, preferred_element_type=jnp.float32)  9.49 us
    dot_general x1, matrix products, local(): jnp.dot(picks, features, preferred_element_type=jnp.float32)  9.18 us
  transfers between devices with their start and end apart: 4, of which 2 were waited for; matrix products, arithmetic and copies ran while one was open for 59% of the time, Pallas kernels for 0%

profile of v2, /device:TPU:0, one launch (start us, length us, event | category | flops | bytes accessed | tf_op | source)
XLA Modules:
  0.0 328.6 jit_solution(11105818809127448490)
XLA Ops:
  7.2 0.7 compare_select_fusion
  8.4 1.2 gather_fusion
  9.7 0.7 iota_compare_fusion.18
  10.4 0.7 copy.11
  11.2 9.2 %fusion.10 = bf16[4096,256]{1,0:T(8,128)(2,1)} fusion(bf16[2048,256]{1,0:T(8,128)(2,1)S(1)} %copy-done, s32[4096]{0:T(1024)S(1)} %bitcast.84, pred[4096]{0:T(1024)(128)(4,1)S(1)} %lt.28), kind=kOutput, calls=%fused_computation.31 | convolution fusion | flops 4312793088 | bytes 3166208 | tf_op jit(solution)/shard_map/dot_general | solution.py:43
  20.3 7.1 %all-to-all-start = ((bf16[16,256,256]{2,1,0:T(8,128)(2,1)}), bf16[16,256,256]{2,1,0:T(8,128)(2,1)S(1)}, u32[]{:S(2)}, u32[]{:S(2)}) async-start(bf16[16,256,256]{2,1,0:T(8,128)(2,1)} %bitcast.49), calls=%async_computation | async-start | bytes 4194304 | tf_op jit(solution)/shard_map/all_to_all | solution.py:45
  27.6 107.5 %add_convert_fusion = (bf16[2048,4096]{1,0:T(8,128)(2,1)}, bf16[2048,4096]{1,0:T(8,128)(2,1)}) fusion(s32[4096]{0:T(1024)S(1)} %get-tuple-element.28, s32[2048]{0:T(1024)S(1)} %bitcast.79, s32[2048]{0:T(1024)S(1)} %bitcast.81, s32[2048]{0:T(1024)S(1)} %bitcast.53, s32[2048]{0:T(1024)S(1)} %bitcast.55, s32[2048]{0:T(1024)S(1)} %bitcast.57, ...), kind=kLoop, calls=%fused_computation.4 | loop fusion | flops 805306368 | bytes 33718272 | tf_op jit(solution)/shard_map/convert_element_type | solution.py:19
  135.2 40.4 %add_convert_fusion.2 = bf16[2048,2048]{1,0:T(8,128)(2,1)} fusion(s32[2048]{0:T(1024)S(1)} %bitcast.80, s32[2048]{0:T(1024)S(1)} %bitcast.82, s32[2048]{0:T(1024)S(1)} %bitcast.54, s32[2048]{0:T(1024)S(1)} %bitcast.56, s32[2048]{0:T(1024)S(1)} %bitcast.58, s32[2048]{0:T(1024)S(1)} %bitcast.60, s32[2048]{0:T(1024)S(1)} %bitcast.62, s32[2048]{0:T(1024)S(1)} %bitcast.64, ...), kind=kLoop, calls=%fused_computation.12 | loop fusion | flops 201326592 | bytes 8519680 | tf_op jit(solution)/shard_map/convert_element_type | solution.py:19
  175.5 1.8 fusion.39
  177.3 9.5 %fusion.40 = f32[2048,256]{1,0:T(8,128)} fusion(bf16[2048,4096]{1,0:T(8,128)(2,1)} %get-tuple-element.6, bf16[4096,256]{1,0:T(8,128)(2,1)S(1)} %bitcast.48), kind=kOutput, calls=%fused_computation.70 | convolution fusion | flops 4294967296 | bytes 20971520 | tf_op jit(solution)/shard_map/dot_general | solution.py:58
  186.8 12.4 %fusion.41 = f32[2048,256]{1,0:T(8,128)} fusion(bf16[2048,4096]{1,0:T(8,128)(2,1)} %get-tuple-element.7, bf16[4096,256]{1,0:T(8,128)(2,1)} %all-gather.3.cloned.1.call-done), kind=kOutput, calls=%fused_computation.71 | convolution fusion | flops 4294967296 | bytes 20971520 | tf_op jit(solution)/shard_map/dot_general | solution.py:59
  199.2 10.8 %fusion.28 = (bf16[2048,256]{1,0:T(8,128)(2,1)S(1)}, bf16[2048,256]{1,0:T(8,128)(2,1)}) fusion(bf16[2048,256]{1,0:T(8,128)(2,1)} %param.17, f32[256]{0:T(256)S(1)} %copy-done.7, f32[2048,256]{1,0:T(8,128)} %fusion.39, bf16[256,256]{1,0:T(8,128)(2,1)S(1)} %copy-done.3, f32[2048,256]{1,0:T(8,128)} %fusion.41, f32[2048,256]{1,0:T(8,128)} %fusion.40, ...), kind=kOutput, calls=%fused_computation.52 | convolution fusion | flops 2431123456 | bytes 19006464 | tf_op jit(solution)/shard_map/dot_general | solution.py:62
  210.4 9.8 %convolution_convert_fusion = bf16[4096,256]{1,0:T(8,128)(2,1)} fusion(bf16[2048,4096]{1,0:T(8,128)(2,1)} %get-tuple-element.6, bf16[2048,256]{1,0:T(8,128)(2,1)S(1)} %fusion.25), kind=kOutput, calls=%fused_computation.32 | convolution fusion | flops 4296015872 | bytes 19922944 | tf_op jit(solution)/shard_map/dot_general | solution.py:23
  220.2 7.2 %all-to-all-start.1 = ((bf16[16,256,256]{2,1,0:T(8,128)(2,1)}), bf16[16,256,256]{2,1,0:T(8,128)(2,1)}, u32[]{:S(2)}, u32[]{:S(2)}) async-start(bf16[16,256,256]{2,1,0:T(8,128)(2,1)} %bitcast.50), calls=%async_computation.1 | async-start | bytes 4194304 | tf_op jit(solution)/shard_map/all_to_all | solution.py:83
  227.5 10.2 %fusion.43 = f32[4096,256]{1,0:T(8,128)} fusion(bf16[2048,4096]{1,0:T(8,128)(2,1)} %get-tuple-element.7, bf16[2048,256]{1,0:T(8,128)(2,1)S(1)} %fusion.25), kind=kOutput, calls=%fused_computation.73 | convolution fusion | flops 4294967296 | bytes 22020096 | tf_op jit(solution)/shard_map/dot_general | solution.py:23
  237.7 19.2 %all-to-all-done.1 = bf16[16,256,256]{2,1,0:T(8,128)(2,1)} async-done(((bf16[16,256,256]{2,1,0:T(8,128)(2,1)}), bf16[16,256,256]{2,1,0:T(8,128)(2,1)}, u32[]{:S(2)}, u32[]{:S(2)}) %all-to-all-start.1) | async-done | bytes 2097184 | tf_op jit(solution)/shard_map/all_to_all | solution.py:83
  256.9 8.5 %all-to-all-start.2 = ((f32[128,32,256]{2,1,0:T(8,128)}), f32[128,32,256]{2,1,0:T(8,128)}, u32[]{:S(2)}, u32[]{:S(2)}) async-start(f32[128,32,256]{2,1,0:T(8,128)} %bitcast.47), calls=%async_computation.2 | async-start | bytes 8388608 | tf_op jit(solution)/shard_map/all_to_all | solution.py:73
  265.4 6.0 %fusion.42 = f32[2048,256]{1,0:T(8,128)S(1)} fusion(bf16[2048,2048]{1,0:T(8,128)(2,1)} %add_convert_fusion.2, bf16[2048,256]{1,0:T(8,128)(2,1)S(1)} %fusion.25), kind=kOutput, calls=%fused_computation.72 | convolution fusion | flops 2147483648 | bytes 11534336 | tf_op jit(solution)/shard_map/dot_general | solution.py:23
  271.4 0.5 convolution_add_fusion
  271.9 8.7 %fusion.16 = f32[2048,256]{1,0:T(8,128)S(1)} fusion(f32[2048,256]{1,0:T(8,128)S(1)} %convolution_add_fusion, bf16[16,256,256]{2,1,0:T(8,128)(2,1)} %all-to-all-done.1, s32[16,256]{1,0:T(8,128)S(1)} %copy-done.6, pred[16,256]{1,0:T(8,128)(4,1)S(1)} %iota_compare_fusion.18), kind=kOutput, calls=%fused_computation.36 | convolution fusion | flops 4312268800 | bytes 6311936 | tf_op jit(solution)/shard_map/dot_general | solution.py:23
  280.6 35.9 %all-to-all-done.2 = f32[128,32,256]{2,1,0:T(8,128)} async-done(((f32[128,32,256]{2,1,0:T(8,128)}), f32[128,32,256]{2,1,0:T(8,128)}, u32[]{:S(2)}, u32[]{:S(2)}) %all-to-all-start.2) | async-done | bytes 4194336 | tf_op jit(solution)/shard_map/all_to_all | solution.py:73
  316.5 2.5 reduce_sum.9
  318.9 1.5 scatter_fusion
  320.5 1.3 copy-done.5
  (24 shorter events, 1.1 us)
Async XLA Ops:
  7.2 1.2 copy-start
  7.2 179.6 %all-gather.3.cloned.1.call-start = ((), (), s32[]{:S(2)}) async-start(), calls=%async_computation.3 | async-start | bytes 2113536 | tf_op jit(solution)/shard_map/all_gather | solution.py:48
  11.1 16.4 %copy-start.4 = (s32[2048,16]{0,1:T(8,128)S(1)}, s32[2048,16]{0,1:T(8,128)}, u32[]{:S(2)}) copy-start(s32[2048,16]{0,1:T(8,128)} %param.13) | copy-start | bytes 393220
  20.3 157.0 %all-to-all-start = ((bf16[16,256,256]{2,1,0:T(8,128)(2,1)}), bf16[16,256,256]{2,1,0:T(8,128)(2,1)S(1)}, u32[]{:S(2)}, u32[]{:S(2)}) async-start(bf16[16,256,256]{2,1,0:T(8,128)(2,1)} %bitcast.49), calls=%async_computation | async-start | bytes 4194304 | tf_op jit(solution)/shard_map/all_to_all | solution.py:45
  27.6 147.9 %copy-start.2 = (bf16[256,256]{1,0:T(8,128)(2,1)S(1)}, bf16[256,256]{1,0:T(8,128)(2,1)}, u32[]{:S(2)}) copy-start(bf16[256,256]{1,0:T(8,128)(2,1)} %param.14) | copy-start | bytes 393220
  186.8 12.4 %copy-start.3 = (bf16[256,256]{1,0:T(8,128)(2,1)S(1)}, bf16[256,256]{1,0:T(8,128)(2,1)}, u32[]{:S(2)}) copy-start(bf16[256,256]{1,0:T(8,128)(2,1)} %param.15) | copy-start | bytes 393220
  186.8 12.4 %copy-start.7 = (f32[256]{0:T(256)S(1)}, f32[256]{0:T(256)}, u32[]{:S(2)}) copy-start(f32[256]{0:T(256)} %param.16) | copy-start | bytes 3076
  220.2 36.7 %all-to-all-start.1 = ((bf16[16,256,256]{2,1,0:T(8,128)(2,1)}), bf16[16,256,256]{2,1,0:T(8,128)(2,1)}, u32[]{:S(2)}, u32[]{:S(2)}) async-start(bf16[16,256,256]{2,1,0:T(8,128)(2,1)} %bitcast.50), calls=%async_computation.1 | async-start | bytes 4194304 | tf_op jit(solution)/shard_map/all_to_all | solution.py:83
  237.7 34.2 %copy-start.6 = (s32[16,256]{1,0:T(8,128)S(1)}, s32[16,256]{1,0:T(8,128)}, u32[]{:S(2)}) copy-start(s32[16,256]{1,0:T(8,128)} %param.10) | copy-start | bytes 49156
  256.9 59.6 %all-to-all-start.2 = ((f32[128,32,256]{2,1,0:T(8,128)}), f32[128,32,256]{2,1,0:T(8,128)}, u32[]{:S(2)}, u32[]{:S(2)}) async-start(f32[128,32,256]{2,1,0:T(8,128)} %bitcast.47), calls=%async_computation.2 | async-start | bytes 8388608 | tf_op jit(solution)/shard_map/all_to_all | solution.py:73
  271.4 50.4 %copy-start.1 = (bf16[2048,256]{1,0:T(8,128)(2,1)S(1)}, bf16[2048,256]{1,0:T(8,128)(2,1)}, u32[]{:S(2)}) copy-start(bf16[2048,256]{1,0:T(8,128)(2,1)} %param.9) | copy-start | bytes 3145732
  320.5 1.3 copy-start.5
Sparse Core Ops, SparseCore 0:
  11.5 86.6 all-gather.2

commit v3 on v2

--- a/solution.py
+++ b/solution.py
@@ -10,13 +10,14 @@
 
 def count_matrix(index_rows, start, width):
     degree = index_rows.shape[1]
-    column_ids = jnp.arange(start, start + width, dtype=jnp.int32)
-    counts = (index_rows[:, 0:1] == column_ids[None, :]).astype(jnp.float32)
+    narrow_rows = index_rows.astype(jnp.int16)
+    column_ids = jnp.arange(start, start + width, dtype=jnp.int16)
+    counts = (narrow_rows[:, 0:1] == column_ids[None, :]).astype(jnp.bfloat16)
     for slot in range(1, degree):
-        counts = counts + (index_rows[:, slot : slot + 1] == column_ids[None, :]).astype(
-            jnp.float32
+        counts = counts + (narrow_rows[:, slot : slot + 1] == column_ids[None, :]).astype(
+            jnp.bfloat16
         )
-    return counts.astype(jnp.bfloat16)
+    return counts
 
 
 def transposed_dot(counts, values):

time: 331 us -> 324 us (0.979)
  other arithmetic: 153 us -> 147 us
    convert_element_type x2 -> x1, other arithmetic: 148 us -> 0.01 us  [count_matrix(): narrow_rows = index_rows.astype(jnp.int16)]
    add x1 -> x3, other arithmetic: 0.01 us -> 141 us  [the longest x2 141 us: count_matrix(): counts + (narrow_rows[:, slot:slot + 1] == column_ids[None, :]).astype(jn...]
where the time goes in v3:
time: 324 us; the launch traced here: 322 us
  other arithmetic  147 us (45%)
  matrix products  79.3 us (24%)
  waiting for transfers between devices  54.9 us (17%)
  starting transfers between devices  23 us (7%)
  between operations  14.2 us (4%)
  local copies, waits for them, and re-layouts  4.12 us (1%)
    add x2, other arithmetic, count_matrix(): counts + (narrow_rows[:, slot:slot + 1] == column_ids[None, :]).astype(jn...  141 us
    all_to_all x1, waiting for transfers between devices, local(): lax.all_to_all(hub_back.reshape(device_count, hub_count, feature_width),...  35.8 us
    dot_general x4, matrix products, transposed_dot(): lax.dot_general(counts, values, (((0,), (0,)), ((), ())), preferred_eleme...  34.8 us
    all_to_all x1, waiting for transfers between devices, local(): lax.all_to_all(halo_back.astype(jnp.bfloat16).reshape(peer_count, slot_co...  19.1 us
    dot_general x1, matrix products, local(): jnp.dot(counts_hub, hub_table, preferred_element_type=jnp.float32)  12.4 us
    dot_general x1, matrix products, local(): jnp.dot(aggregated, w_neigh, preferred_element_type=jnp.float32)  10.8 us
    dot_general x1, matrix products, local(): jnp.dot(counts_halo, incoming, preferred_element_type=jnp.float32)  9.48 us
    dot_general x1, matrix products, local(): jnp.dot(picks, features, preferred_element_type=jnp.float32)  9.18 us
  transfers between devices with their start and end apart: 4, of which 2 were waited for; matrix products, arithmetic and copies ran while one was open for 59% of the time, Pallas kernels for 0%

profile of v3, /device:TPU:0, one launch (start us, length us, event | category | flops | bytes accessed | tf_op | source)
XLA Modules:
  0.0 322.4 jit_solution(18400754529142828573)
XLA Ops:
  7.2 0.7 compare_select_fusion
  8.4 1.2 gather_fusion
  9.7 0.7 iota_compare_fusion.2
  10.4 0.7 copy.11
  11.2 9.2 %fusion.55 = bf16[4096,256]{1,0:T(8,128)(2,1)} fusion(bf16[2048,256]{1,0:T(8,128)(2,1)S(1)} %copy-done, s32[4096]{0:T(1024)S(1)} %bitcast.36, pred[4096]{0:T(1024)(128)(4,1)S(1)} %lt.28), kind=kOutput, calls=%fused_computation.105 | convolution fusion | flops 4312793088 | bytes 3166208 | tf_op jit(solution)/shard_map/dot_general | solution.py:44
  20.3 7.1 %all-to-all-start = ((bf16[16,256,256]{2,1,0:T(8,128)(2,1)}), bf16[16,256,256]{2,1,0:T(8,128)(2,1)S(1)}, u32[]{:S(2)}, u32[]{:S(2)}) async-start(bf16[16,256,256]{2,1,0:T(8,128)(2,1)} %bitcast.33), calls=%async_computation | async-start | bytes 4194304 | tf_op jit(solution)/shard_map/all_to_all | solution.py:46
  27.9 108.5 %fusion.35 = (bf16[2048,4096]{1,0:T(8,128)(2,1)}, bf16[2048,4096]{1,0:T(8,128)(2,1)}) fusion(s16[4096]{0:T(1024)(128)(2,1)S(1)} %get-tuple-element.28, s16[2048]{0:T(1024)(128)(2,1)S(1)} %get-tuple-element.9, s16[2048]{0:T(1024)(128)(2,1)S(1)} %get-tuple-element.10, s16[2048]{0:T(1024)(128)(2,1)S(1)} %get-tuple-element.11, ...), kind=kLoop, calls=%fused_computation.69 | loop fusion | flops 788529152 | bytes 33636352 | tf_op jit(solution)/shard_map/add | solution.py:17
  136.4 32.9 %fusion.54 = bf16[2048,2048]{1,0:T(8,128)(2,1)} fusion(s16[2048]{0:T(1024)(128)(2,1)S(1)} %get-tuple-element.9, s16[2048]{0:T(1024)(128)(2,1)S(1)} %get-tuple-element.10, s16[2048]{0:T(1024)(128)(2,1)S(1)} %get-tuple-element.11, s16[2048]{0:T(1024)(128)(2,1)S(1)} %get-tuple-element.12, s16[2048]{0:T(1024)(128)(2,1)S(1)} %get-tuple-element.13, ...), kind=kLoop, calls=%fused_computation.104 | loop fusion | flops 268435456 | bytes 8454144 | tf_op jit(solution)/shard_map/add | solution.py:17
  169.3 1.8 fusion.83
  171.0 9.5 %fusion.84 = f32[2048,256]{1,0:T(8,128)} fusion(bf16[2048,4096]{1,0:T(8,128)(2,1)} %get-tuple-element.6, bf16[4096,256]{1,0:T(8,128)(2,1)S(1)} %bitcast.32), kind=kOutput, calls=%fused_computation.159 | convolution fusion | flops 4294967296 | bytes 20971520 | tf_op jit(solution)/shard_map/dot_general | solution.py:59
  180.5 12.4 %fusion.85 = f32[2048,256]{1,0:T(8,128)} fusion(bf16[2048,4096]{1,0:T(8,128)(2,1)} %get-tuple-element.7, bf16[4096,256]{1,0:T(8,128)(2,1)} %all-gather.3.cloned.1.call-done), kind=kOutput, calls=%fused_computation.160 | convolution fusion | flops 4294967296 | bytes 20971520 | tf_op jit(solution)/shard_map/dot_general | solution.py:60
  192.9 10.8 %fusion.73 = (bf16[2048,256]{1,0:T(8,128)(2,1)S(1)}, bf16[2048,256]{1,0:T(8,128)(2,1)}) fusion(bf16[2048,256]{1,0:T(8,128)(2,1)} %param.17, f32[256]{0:T(256)S(1)} %copy-done.7, f32[2048,256]{1,0:T(8,128)} %fusion.83, bf16[256,256]{1,0:T(8,128)(2,1)S(1)} %copy-done.3, f32[2048,256]{1,0:T(8,128)} %fusion.85, f32[2048,256]{1,0:T(8,128)} %fusion.84, ...), kind=kOutput, calls=%fused_computation.126 | convolution fusion | flops 2431123456 | bytes 19006464 | tf_op jit(solution)/shard_map/dot_general | solution.py:63
  204.2 9.8 %convolution_convert_fusion = bf16[4096,256]{1,0:T(8,128)(2,1)} fusion(bf16[2048,4096]{1,0:T(8,128)(2,1)} %get-tuple-element.6, bf16[2048,256]{1,0:T(8,128)(2,1)S(1)} %fusion.70), kind=kOutput, calls=%fused_computation.106 | convolution fusion | flops 4296015872 | bytes 19922944 | tf_op jit(solution)/shard_map/dot_general | solution.py:24
  214.0 7.3 %all-to-all-start.1 = ((bf16[16,256,256]{2,1,0:T(8,128)(2,1)}), bf16[16,256,256]{2,1,0:T(8,128)(2,1)}, u32[]{:S(2)}, u32[]{:S(2)}) async-start(bf16[16,256,256]{2,1,0:T(8,128)(2,1)} %bitcast.34), calls=%async_computation.1 | async-start | bytes 4194304 | tf_op jit(solution)/shard_map/all_to_all | solution.py:84
  221.2 10.2 %fusion.87 = f32[4096,256]{1,0:T(8,128)} fusion(bf16[2048,4096]{1,0:T(8,128)(2,1)} %get-tuple-element.7, bf16[2048,256]{1,0:T(8,128)(2,1)S(1)} %fusion.70), kind=kOutput, calls=%fused_computation.162 | convolution fusion | flops 4294967296 | bytes 22020096 | tf_op jit(solution)/shard_map/dot_general | solution.py:24
  231.5 19.1 %all-to-all-done.1 = bf16[16,256,256]{2,1,0:T(8,128)(2,1)} async-done(((bf16[16,256,256]{2,1,0:T(8,128)(2,1)}), bf16[16,256,256]{2,1,0:T(8,128)(2,1)}, u32[]{:S(2)}, u32[]{:S(2)}) %all-to-all-start.1) | async-done | bytes 2097184 | tf_op jit(solution)/shard_map/all_to_all | solution.py:84
  250.6 8.5 %all-to-all-start.2 = ((f32[128,32,256]{2,1,0:T(8,128)}), f32[128,32,256]{2,1,0:T(8,128)}, u32[]{:S(2)}, u32[]{:S(2)}) async-start(f32[128,32,256]{2,1,0:T(8,128)} %bitcast.31), calls=%async_computation.2 | async-start | bytes 8388608 | tf_op jit(solution)/shard_map/all_to_all | solution.py:74
  259.1 6.0 %fusion.86 = f32[2048,256]{1,0:T(8,128)S(1)} fusion(bf16[2048,2048]{1,0:T(8,128)(2,1)} %fusion.54, bf16[2048,256]{1,0:T(8,128)(2,1)S(1)} %fusion.70), kind=kOutput, calls=%fused_computation.161 | convolution fusion | flops 2147483648 | bytes 11534336 | tf_op jit(solution)/shard_map/dot_general | solution.py:24
  265.1 0.5 convolution_add_fusion
  265.7 8.8 %fusion.61 = f32[2048,256]{1,0:T(8,128)S(1)} fusion(f32[2048,256]{1,0:T(8,128)S(1)} %convolution_add_fusion, bf16[16,256,256]{2,1,0:T(8,128)(2,1)} %all-to-all-done.1, s32[16,256]{1,0:T(8,128)S(1)} %copy-done.6, pred[16,256]{1,0:T(8,128)(4,1)S(1)} %iota_compare_fusion.2), kind=kOutput, calls=%fused_computation.110 | convolution fusion | flops 4312268800 | bytes 6311936 | tf_op jit(solution)/shard_map/dot_general | solution.py:24
  274.4 35.8 %all-to-all-done.2 = f32[128,32,256]{2,1,0:T(8,128)} async-done(((f32[128,32,256]{2,1,0:T(8,128)}), f32[128,32,256]{2,1,0:T(8,128)}, u32[]{:S(2)}, u32[]{:S(2)}) %all-to-all-start.2) | async-done | bytes 4194336 | tf_op jit(solution)/shard_map/all_to_all | solution.py:74
  310.2 2.5 reduce_sum.9
  312.6 1.5 scatter_fusion
  314.2 1.3 copy-done.5
  (25 shorter events, 1.4 us)
Async XLA Ops:
  7.2 1.2 copy-start
  7.2 173.4 %all-gather.3.cloned.1.call-start = ((), (), s32[]{:S(2)}) async-start(), calls=%async_computation.3 | async-start | bytes 2113536 | tf_op jit(solution)/shard_map/all_gather | solution.py:49
  11.1 16.4 %copy-start.4 = (s32[2048,16]{0,1:T(8,128)S(1)}, s32[2048,16]{0,1:T(8,128)}, u32[]{:S(2)}) copy-start(s32[2048,16]{0,1:T(8,128)} %param.13) | copy-start | bytes 393220
  20.3 150.7 %all-to-all-start = ((bf16[16,256,256]{2,1,0:T(8,128)(2,1)}), bf16[16,256,256]{2,1,0:T(8,128)(2,1)S(1)}, u32[]{:S(2)}, u32[]{:S(2)}) async-start(bf16[16,256,256]{2,1,0:T(8,128)(2,1)} %bitcast.33), calls=%async_computation | async-start | bytes 4194304 | tf_op jit(solution)/shard_map/all_to_all | solution.py:46
  136.4 32.9 %copy-start.2 = (bf16[256,256]{1,0:T(8,128)(2,1)S(1)}, bf16[256,256]{1,0:T(8,128)(2,1)}, u32[]{:S(2)}) copy-start(bf16[256,256]{1,0:T(8,128)(2,1)} %param.14) | copy-start | bytes 393220
  180.5 12.4 %copy-start.3 = (bf16[256,256]{1,0:T(8,128)(2,1)S(1)}, bf16[256,256]{1,0:T(8,128)(2,1)}, u32[]{:S(2)}) copy-start(bf16[256,256]{1,0:T(8,128)(2,1)} %param.15) | copy-start | bytes 393220
  180.5 12.4 %copy-start.7 = (f32[256]{0:T(256)S(1)}, f32[256]{0:T(256)}, u32[]{:S(2)}) copy-start(f32[256]{0:T(256)} %param.16) | copy-start | bytes 3076
  214.0 36.6 %all-to-all-start.1 = ((bf16[16,256,256]{2,1,0:T(8,128)(2,1)}), bf16[16,256,256]{2,1,0:T(8,128)(2,1)}, u32[]{:S(2)}, u32[]{:S(2)}) async-start(bf16[16,256,256]{2,1,0:T(8,128)(2,1)} %bitcast.34), calls=%async_computation.1 | async-start | bytes 4194304 | tf_op jit(solution)/shard_map/all_to_all | solution.py:84
  250.6 59.6 %all-to-all-start.2 = ((f32[128,32,256]{2,1,0:T(8,128)}), f32[128,32,256]{2,1,0:T(8,128)}, u32[]{:S(2)}, u32[]{:S(2)}) async-start(f32[128,32,256]{2,1,0:T(8,128)} %bitcast.31), calls=%async_computation.2 | async-start | bytes 8388608 | tf_op jit(solution)/shard_map/all_to_all | solution.py:74
  259.1 6.5 %copy-start.6 = (s32[16,256]{1,0:T(8,128)S(1)}, s32[16,256]{1,0:T(8,128)}, u32[]{:S(2)}) copy-start(s32[16,256]{1,0:T(8,128)} %param.10) | copy-start | bytes 49156
  265.6 49.9 %copy-start.1 = (bf16[2048,256]{1,0:T(8,128)(2,1)S(1)}, bf16[2048,256]{1,0:T(8,128)(2,1)}, u32[]{:S(2)}) copy-start(bf16[2048,256]{1,0:T(8,128)(2,1)} %param.9) | copy-start | bytes 3145732
  314.2 1.3 copy-start.5
Sparse Core Ops, SparseCore 0:
  11.5 86.6 all-gather.2

commit v4 on v3

--- a/solution.py
+++ b/solution.py
@@ -46,7 +46,9 @@
     incoming = lax.all_to_all(outgoing, "col", split_axis=0, concat_axis=0, tiled=True)
     incoming = incoming.reshape(-1, feature_width)
     hub_local = features[hub_rows]
-    hub_table = lax.all_gather(hub_local, ("row", "col"), axis=0, tiled=True)
+    hub_copies = jnp.broadcast_to(hub_local[None], (device_count, hub_count, feature_width))
+    hub_table = lax.all_to_all(hub_copies, ("row", "col"), split_axis=0, concat_axis=0, tiled=True)
+    hub_table = hub_table.reshape(device_count * hub_count, feature_width)
 
     counts_own = count_matrix(neighbours, 0, vertex_count)
     counts_halo = count_matrix(neighbours, vertex_count, halo_width)

time: 324 us -> 323 us (level)
  between operations: 14.2 us -> 0.84 us
  starting transfers between devices: 23 us -> 32.8 us
    all_to_all x0 -> x1, starting transfers between devices: none -> 12 us  [local(): lax.all_to_all(hub_copies, ('row', 'col'), split_axis=0, concat_axis=0, t...]
  transfers between devices with their start and end apart: 4 -> 4, of which waited for: 2 -> 2; matrix products, arithmetic and copies ran while one was open for 59% -> 56% of each run, Pallas kernels for 0% -> 0%
where the time goes in v4:
time: 323 us; the launch traced here: 321 us
  other arithmetic  146 us (45%)
  matrix products  79.3 us (25%)
  waiting for transfers between devices  56.8 us (18%)
  starting transfers between devices  32.8 us (10%)
  local copies, waits for them, and re-layouts  4.63 us (1%)
    add x2, other arithmetic, count_matrix(): counts + (narrow_rows[:, slot:slot + 1] == column_ids[None, :]).astype(jn...  141 us
    all_to_all x1, waiting for transfers between devices, local(): lax.all_to_all(hub_back.reshape(device_count, hub_count, feature_width),...  35.8 us
    dot_general x4, matrix products, transposed_dot(): lax.dot_general(counts, values, (((0,), (0,)), ((), ())), preferred_eleme...  34.8 us
    all_to_all x1, waiting for transfers between devices, local(): lax.all_to_all(halo_back.astype(jnp.bfloat16).reshape(peer_count, slot_co...  21 us
    dot_general x1, matrix products, local(): jnp.dot(counts_hub, hub_table, preferred_element_type=jnp.float32)  12.4 us
    all_to_all x1, starting transfers between devices, local(): lax.all_to_all(hub_copies, ('row', 'col'), split_axis=0, concat_axis=0, t...  12 us
    dot_general x1, matrix products, local(): jnp.dot(aggregated, w_neigh, preferred_element_type=jnp.float32)  10.8 us
    dot_general x1, matrix products, local(): jnp.dot(counts_halo, incoming, preferred_element_type=jnp.float32)  9.47 us
  transfers between devices with their start and end apart: 4, of which 2 were waited for; matrix products, arithmetic and copies ran while one was open for 56% of the time, Pallas kernels for 0%

profile of v4, /device:TPU:0, one launch (start us, length us, event | category | flops | bytes accessed | tf_op | source)
XLA Modules:
  0.0 320.5 jit_solution(6792847410317597769)
XLA Ops:
  0.6 0.8 iota_compare_fusion.2
  1.5 0.7 copy.11
  2.2 9.2 %fusion.55 = bf16[4096,256]{1,0:T(8,128)(2,1)} fusion(bf16[2048,256]{1,0:T(8,128)(2,1)S(1)} %copy-done, s32[4096]{0:T(1024)S(1)} %bitcast.37, pred[4096]{0:T(1024)(128)(4,1)S(1)} %lt.28), kind=kOutput, calls=%fused_computation.105 | convolution fusion | flops 4312793088 | bytes 3166208 | tf_op jit(solution)/shard_map/dot_general | solution.py:44
  11.4 7.1 %all-to-all-start = ((bf16[16,256,256]{2,1,0:T(8,128)(2,1)}), bf16[16,256,256]{2,1,0:T(8,128)(2,1)S(1)}, u32[]{:S(2)}, u32[]{:S(2)}) async-start(bf16[16,256,256]{2,1,0:T(8,128)(2,1)} %bitcast.34), calls=%async_computation | async-start | bytes 4194304 | tf_op jit(solution)/shard_map/all_to_all | solution.py:46
  19.0 108.5 %fusion.35 = (bf16[2048,4096]{1,0:T(8,128)(2,1)}, bf16[2048,4096]{1,0:T(8,128)(2,1)}) fusion(s16[4096]{0:T(1024)(128)(2,1)S(1)} %get-tuple-element.28, s16[2048]{0:T(1024)(128)(2,1)S(1)} %get-tuple-element.9, s16[2048]{0:T(1024)(128)(2,1)S(1)} %get-tuple-element.10, s16[2048]{0:T(1024)(128)(2,1)S(1)} %get-tuple-element.11, ...), kind=kLoop, calls=%fused_computation.69 | loop fusion | flops 788529152 | bytes 33636352 | tf_op jit(solution)/shard_map/add | solution.py:17
  127.5 0.6 gather_fusion
  128.2 1.5 broadcast_in_dim.5
  129.7 12.0 %all-to-all-start.1 = ((bf16[128,32,256]{2,1,0:T(8,128)(2,1)}), bf16[128,32,256]{2,1,0:T(8,128)(2,1)}, u32[]{:S(2)}, u32[]{:S(2)}) async-start(bf16[128,32,256]{2,1,0:T(8,128)(2,1)} %broadcast_in_dim.5), calls=%async_computation.1 | async-start | bytes 4194304 | tf_op jit(solution)/shard_map/all_to_all | solution.py:50
  141.7 32.9 %fusion.54 = bf16[2048,2048]{1,0:T(8,128)(2,1)} fusion(s16[2048]{0:T(1024)(128)(2,1)S(1)} %get-tuple-element.9, s16[2048]{0:T(1024)(128)(2,1)S(1)} %get-tuple-element.10, s16[2048]{0:T(1024)(128)(2,1)S(1)} %get-tuple-element.11, s16[2048]{0:T(1024)(128)(2,1)S(1)} %get-tuple-element.12, s16[2048]{0:T(1024)(128)(2,1)S(1)} %get-tuple-element.13, ...), kind=kLoop, calls=%fused_computation.104 | loop fusion | flops 268435456 | bytes 8454144 | tf_op jit(solution)/shard_map/add | solution.py:17
  174.6 1.8 fusion.83
  176.3 9.5 %fusion.84 = f32[2048,256]{1,0:T(8,128)} fusion(bf16[2048,4096]{1,0:T(8,128)(2,1)} %get-tuple-element.6, bf16[4096,256]{1,0:T(8,128)(2,1)S(1)} %bitcast.33), kind=kOutput, calls=%fused_computation.159 | convolution fusion | flops 4294967296 | bytes 20971520 | tf_op jit(solution)/shard_map/dot_general | solution.py:61
  185.8 12.4 %fusion.85 = f32[2048,256]{1,0:T(8,128)} fusion(bf16[2048,4096]{1,0:T(8,128)(2,1)} %get-tuple-element.7, bf16[4096,256]{1,0:T(8,128)(2,1)} %bitcast.2), kind=kOutput, calls=%fused_computation.160 | convolution fusion | flops 4294967296 | bytes 20971520 | tf_op jit(solution)/shard_map/dot_general | solution.py:62
  198.2 10.8 %fusion.73 = (bf16[2048,256]{1,0:T(8,128)(2,1)S(1)}, bf16[2048,256]{1,0:T(8,128)(2,1)}) fusion(bf16[2048,256]{1,0:T(8,128)(2,1)} %param.17, f32[256]{0:T(256)S(1)} %copy-done.7, f32[2048,256]{1,0:T(8,128)} %fusion.83, bf16[256,256]{1,0:T(8,128)(2,1)S(1)} %copy-done.3, f32[2048,256]{1,0:T(8,128)} %fusion.85, f32[2048,256]{1,0:T(8,128)} %fusion.84, ...), kind=kOutput, calls=%fused_computation.126 | convolution fusion | flops 2431123456 | bytes 19006464 | tf_op jit(solution)/shard_map/dot_general | solution.py:65
  209.4 9.8 %convolution_convert_fusion = bf16[4096,256]{1,0:T(8,128)(2,1)} fusion(bf16[2048,4096]{1,0:T(8,128)(2,1)} %get-tuple-element.6, bf16[2048,256]{1,0:T(8,128)(2,1)S(1)} %fusion.70), kind=kOutput, calls=%fused_computation.106 | convolution fusion | flops 4296015872 | bytes 19922944 | tf_op jit(solution)/shard_map/dot_general | solution.py:24
  219.3 6.1 %all-to-all-start.2 = ((bf16[16,256,256]{2,1,0:T(8,128)(2,1)}), bf16[16,256,256]{2,1,0:T(8,128)(2,1)}, u32[]{:S(2)}, u32[]{:S(2)}) async-start(bf16[16,256,256]{2,1,0:T(8,128)(2,1)} %bitcast.35), calls=%async_computation.2 | async-start | bytes 4194304 | tf_op jit(solution)/shard_map/all_to_all | solution.py:86
  225.3 10.2 %fusion.87 = f32[4096,256]{1,0:T(8,128)} fusion(bf16[2048,4096]{1,0:T(8,128)(2,1)} %get-tuple-element.7, bf16[2048,256]{1,0:T(8,128)(2,1)S(1)} %fusion.70), kind=kOutput, calls=%fused_computation.162 | convolution fusion | flops 4294967296 | bytes 22020096 | tf_op jit(solution)/shard_map/dot_general | solution.py:24
  235.5 21.0 %all-to-all-done.2 = bf16[16,256,256]{2,1,0:T(8,128)(2,1)} async-done(((bf16[16,256,256]{2,1,0:T(8,128)(2,1)}), bf16[16,256,256]{2,1,0:T(8,128)(2,1)}, u32[]{:S(2)}, u32[]{:S(2)}) %all-to-all-start.2) | async-done | bytes 2097184 | tf_op jit(solution)/shard_map/all_to_all | solution.py:86
  256.5 7.6 %all-to-all-start.3 = ((f32[128,32,256]{2,1,0:T(8,128)}), f32[128,32,256]{2,1,0:T(8,128)}, u32[]{:S(2)}, u32[]{:S(2)}) async-start(f32[128,32,256]{2,1,0:T(8,128)} %bitcast.32), calls=%async_computation.3 | async-start | bytes 8388608 | tf_op jit(solution)/shard_map/all_to_all | solution.py:76
  264.2 6.0 %fusion.86 = f32[2048,256]{1,0:T(8,128)S(1)} fusion(bf16[2048,2048]{1,0:T(8,128)(2,1)} %fusion.54, bf16[2048,256]{1,0:T(8,128)(2,1)S(1)} %fusion.70), kind=kOutput, calls=%fused_computation.161 | convolution fusion | flops 2147483648 | bytes 11534336 | tf_op jit(solution)/shard_map/dot_general | solution.py:24
  270.7 8.8 %fusion.61 = f32[2048,256]{1,0:T(8,128)S(1)} fusion(f32[2048,256]{1,0:T(8,128)S(1)} %convolution_add_fusion, bf16[16,256,256]{2,1,0:T(8,128)(2,1)} %all-to-all-done.2, s32[16,256]{1,0:T(8,128)S(1)} %copy-done.6, pred[16,256]{1,0:T(8,128)(4,1)S(1)} %iota_compare_fusion.2), kind=kOutput, calls=%fused_computation.110 | convolution fusion | flops 4312268800 | bytes 6311936 | tf_op jit(solution)/shard_map/dot_general | solution.py:24
  279.4 35.8 %all-to-all-done.3 = f32[128,32,256]{2,1,0:T(8,128)} async-done(((f32[128,32,256]{2,1,0:T(8,128)}), f32[128,32,256]{2,1,0:T(8,128)}, u32[]{:S(2)}, u32[]{:S(2)}) %all-to-all-start.3) | async-done | bytes 4194336 | tf_op jit(solution)/shard_map/all_to_all | solution.py:76
  315.2 2.5 reduce_sum.9
  317.7 1.5 scatter_fusion
  319.2 1.3 copy-done.5
  (27 shorter events, 1.4 us)
Async XLA Ops:
  0.6 1.6 copy-start
  2.2 16.4 %copy-start.4 = (s32[2048,16]{0,1:T(8,128)S(1)}, s32[2048,16]{0,1:T(8,128)}, u32[]{:S(2)}) copy-start(s32[2048,16]{0,1:T(8,128)} %param.13) | copy-start | bytes 393220
  11.4 116.7 %all-to-all-start = ((bf16[16,256,256]{2,1,0:T(8,128)(2,1)}), bf16[16,256,256]{2,1,0:T(8,128)(2,1)S(1)}, u32[]{:S(2)}, u32[]{:S(2)}) async-start(bf16[16,256,256]{2,1,0:T(8,128)(2,1)} %bitcast.34), calls=%async_computation | async-start | bytes 4194304 | tf_op jit(solution)/shard_map/all_to_all | solution.py:46
  19.0 108.5 %copy-start.8 = (s32[32]{0:T(128)S(1)}, s32[32]{0:T(128)}, u32[]{:S(2)}) copy-start(s32[32]{0:T(128)} %param.12) | copy-start | bytes 388
  127.5 47.1 %copy-start.2 = (bf16[256,256]{1,0:T(8,128)(2,1)S(1)}, bf16[256,256]{1,0:T(8,128)(2,1)}, u32[]{:S(2)}) copy-start(bf16[256,256]{1,0:T(8,128)(2,1)} %param.14) | copy-start | bytes 393220
  129.7 56.1 %all-to-all-start.1 = ((bf16[128,32,256]{2,1,0:T(8,128)(2,1)}), bf16[128,32,256]{2,1,0:T(8,128)(2,1)}, u32[]{:S(2)}, u32[]{:S(2)}) async-start(bf16[128,32,256]{2,1,0:T(8,128)(2,1)} %broadcast_in_dim.5), calls=%async_computation.1 | async-start | bytes 4194304 | tf_op jit(solution)/shard_map/all_to_all | solution.py:50
  185.8 12.4 %copy-start.3 = (bf16[256,256]{1,0:T(8,128)(2,1)S(1)}, bf16[256,256]{1,0:T(8,128)(2,1)}, u32[]{:S(2)}) copy-start(bf16[256,256]{1,0:T(8,128)(2,1)} %param.15) | copy-start | bytes 393220
  185.8 12.4 %copy-start.7 = (f32[256]{0:T(256)S(1)}, f32[256]{0:T(256)}, u32[]{:S(2)}) copy-start(f32[256]{0:T(256)} %param.16) | copy-start | bytes 3076
  219.3 37.3 %all-to-all-start.2 = ((bf16[16,256,256]{2,1,0:T(8,128)(2,1)}), bf16[16,256,256]{2,1,0:T(8,128)(2,1)}, u32[]{:S(2)}, u32[]{:S(2)}) async-start(bf16[16,256,256]{2,1,0:T(8,128)(2,1)} %bitcast.35), calls=%async_computation.2 | async-start | bytes 4194304 | tf_op jit(solution)/shard_map/all_to_all | solution.py:86
  256.5 58.7 %all-to-all-start.3 = ((f32[128,32,256]{2,1,0:T(8,128)}), f32[128,32,256]{2,1,0:T(8,128)}, u32[]{:S(2)}, u32[]{:S(2)}) async-start(f32[128,32,256]{2,1,0:T(8,128)} %bitcast.32), calls=%async_computation.3 | async-start | bytes 8388608 | tf_op jit(solution)/shard_map/all_to_all | solution.py:76
  264.2 6.5 %copy-start.6 = (s32[16,256]{1,0:T(8,128)S(1)}, s32[16,256]{1,0:T(8,128)}, u32[]{:S(2)}) copy-start(s32[16,256]{1,0:T(8,128)} %param.10) | copy-start | bytes 49156
  270.7 49.9 %copy-start.1 = (bf16[2048,256]{1,0:T(8,128)(2,1)S(1)}, bf16[2048,256]{1,0:T(8,128)(2,1)}, u32[]{:S(2)}) copy-start(bf16[2048,256]{1,0:T(8,128)(2,1)} %param.9) | copy-start | bytes 3145732
  319.2 1.3 copy-start.5

commit v5 on v4

--- a/solution.py
+++ b/solution.py
@@ -43,11 +43,15 @@
     picks = picks.reshape(halo_width, vertex_count)
     outgoing = jnp.dot(picks, features, preferred_element_type=jnp.float32).astype(features.dtype)
     outgoing = outgoing.reshape(peer_count, slot_count, feature_width)
-    incoming = lax.all_to_all(outgoing, "col", split_axis=0, concat_axis=0, tiled=True)
-    incoming = incoming.reshape(-1, feature_width)
     hub_local = features[hub_rows]
-    hub_copies = jnp.broadcast_to(hub_local[None], (device_count, hub_count, feature_width))
-    hub_table = lax.all_to_all(hub_copies, ("row", "col"), split_axis=0, concat_axis=0, tiled=True)
+    hub_copies = jnp.broadcast_to(hub_local[None], (peer_count, hub_count, feature_width))
+    outgoing = jnp.concatenate([outgoing, hub_copies], axis=1)
+    arrived = lax.all_to_all(outgoing, "col", split_axis=0, concat_axis=0, tiled=True)
+    incoming = arrived[:, :slot_count].reshape(-1, feature_width)
+    hub_row_part = arrived[:, slot_count:].reshape(peer_count * hub_count, feature_width)
+    row_count = device_count // peer_count
+    hub_copies = jnp.broadcast_to(hub_row_part[None], (row_count,) + hub_row_part.shape)
+    hub_table = lax.all_to_all(hub_copies, "row", split_axis=0, concat_axis=0, tiled=True)
     hub_table = hub_table.reshape(device_count * hub_count, feature_width)
 
     counts_own = count_matrix(neighbours, 0, vertex_count)

time: 323 us -> 322 us (level)
  other arithmetic: 146 us -> 151 us
  starting transfers between devices: 32.8 us -> 27.8 us
    all_to_all x1, starting transfers between devices: 12 us -> 5.31 us  [local(): lax.all_to_all(hub_copies, 'row', split_axis=0, concat_axis=0, tiled=True)]
  transfers between devices with their start and end apart: 4 -> 4, of which waited for: 2 -> 2; matrix products, arithmetic and copies ran while one was open for 56% -> 57% of each run, Pallas kernels for 0% -> 0%
where the time goes in v5:
time: 322 us; the launch traced here: 320 us
  other arithmetic  151 us (47%)
  matrix products  78.3 us (24%)
  waiting for transfers between devices  56.2 us (17%)
  starting transfers between devices  27.8 us (9%)
  local copies, waits for them, and re-layouts  5.84 us (2%)
    add x2, other arithmetic, count_matrix(): counts + (narrow_rows[:, slot:slot + 1] == column_ids[None, :]).astype(jn...  144 us
    all_to_all x1, waiting for transfers between devices, local(): lax.all_to_all(hub_back.reshape(device_count, hub_count, feature_width),...  35.7 us
    dot_general x4, matrix products, transposed_dot(): lax.dot_general(counts, values, (((0,), (0,)), ((), ())), preferred_eleme...  34.8 us
    all_to_all x1, waiting for transfers between devices, local(): lax.all_to_all(halo_back.astype(jnp.bfloat16).reshape(peer_count, slot_co...  20.5 us
    dot_general x1, matrix products, local(): jnp.dot(counts_hub, hub_table, preferred_element_type=jnp.float32)  12.5 us
    dot_general x1, matrix products, local(): jnp.dot(aggregated, w_neigh, preferred_element_type=jnp.float32)  10.5 us
    dot_general x1, matrix products, local(): jnp.dot(counts_halo, incoming, preferred_element_type=jnp.float32)  9.49 us
    dot_general x1, matrix products, local(): jnp.dot(picks, features, preferred_element_type=jnp.float32)  8.48 us
  transfers between devices with their start and end apart: 4, of which 2 were waited for; matrix products, arithmetic and copies ran while one was open for 57% of the time, Pallas kernels for 0%

profile of v5, /device:TPU:0, one launch (start us, length us, event | category | flops | bytes accessed | tf_op | source)
XLA Modules:
  0.0 319.9 jit_solution(14779816531430210873)
XLA Ops:
  0.6 0.7 compare_select_fusion
  1.4 0.7 iota_compare_fusion.2
  4.1 8.5 %fusion.55 = bf16[4096,256]{1,0:T(8,128)(2,1)S(1)} fusion(bf16[2048,256]{1,0:T(8,128)(2,1)S(1)} %copy-done, s32[4096]{0:T(1024)S(1)} %bitcast.39, pred[4096]{0:T(1024)(128)(4,1)S(1)} %lt.28), kind=kOutput, calls=%fused_computation.105 | convolution fusion | flops 4312793088 | bytes 3166208 | tf_op jit(solution)/shard_map/dot_general | solution.py:44
  12.6 1.6 pad_maximum_fusion
  14.2 7.1 %all-to-all-start = ((bf16[16,288,256]{2,1,0:T(8,128)(2,1)}), bf16[16,288,256]{2,1,0:T(8,128)(2,1)S(1)}, u32[]{:S(2)}, u32[]{:S(2)}) async-start(bf16[16,288,256]{2,1,0:T(8,128)(2,1)} %pad_maximum_fusion), calls=%async_computation | async-start | bytes 4718592 | tf_op jit(solution)/shard_map/all_to_all | solution.py:49
  22.5 108.5 %fusion.35 = (bf16[2048,4096]{1,0:T(8,128)(2,1)}, bf16[2048,4096]{1,0:T(8,128)(2,1)}) fusion(s16[4096]{0:T(1024)(128)(2,1)S(1)} %get-tuple-element.28, s16[2048]{0:T(1024)(128)(2,1)S(1)} %get-tuple-element.9, s16[2048]{0:T(1024)(128)(2,1)S(1)} %get-tuple-element.10, s16[2048]{0:T(1024)(128)(2,1)S(1)} %get-tuple-element.11, ...), kind=kLoop, calls=%fused_computation.69 | loop fusion | flops 788529152 | bytes 33636352 | tf_op jit(solution)/shard_map/add | solution.py:17
  131.0 1.4 broadcast_in_dim.11
  132.4 5.3 %all-to-all-start.1 = ((bf16[8,512,256]{2,1,0:T(8,128)(2,1)}), bf16[8,512,256]{2,1,0:T(8,128)(2,1)}, u32[]{:S(2)}, u32[]{:S(2)}) async-start(bf16[8,512,256]{2,1,0:T(8,128)(2,1)} %broadcast_in_dim.11), calls=%async_computation.1 | async-start | bytes 4194304 | tf_op jit(solution)/shard_map/all_to_all | solution.py:54
  137.8 35.1 %fusion.54 = bf16[2048,2048]{1,0:T(8,128)(2,1)} fusion(s16[2048]{0:T(1024)(128)(2,1)S(1)} %get-tuple-element.9, s16[2048]{0:T(1024)(128)(2,1)S(1)} %get-tuple-element.10, s16[2048]{0:T(1024)(128)(2,1)S(1)} %get-tuple-element.11, s16[2048]{0:T(1024)(128)(2,1)} %copy-done.5, s16[2048]{0:T(1024)(128)(2,1)} %copy-done.6, s16[2048]{0:T(1024)(128)(2,1)} %copy-done.7, ...), kind=kLoop, calls=%fused_computation.104 | loop fusion | flops 268435456 | bytes 8454144 | tf_op jit(solution)/shard_map/add | solution.py:17
  172.8 1.7 fusion.83
  174.7 9.5 %fusion.84 = f32[2048,256]{1,0:T(8,128)} fusion(bf16[2048,4096]{1,0:T(8,128)(2,1)} %get-tuple-element.6, bf16[4096,256]{1,0:T(8,128)(2,1)S(1)} %bitcast.36), kind=kOutput, calls=%fused_computation.160 | convolution fusion | flops 4294967296 | bytes 20971520 | tf_op jit(solution)/shard_map/dot_general | solution.py:65
  184.2 12.5 %fusion.85 = f32[2048,256]{1,0:T(8,128)} fusion(bf16[2048,4096]{1,0:T(8,128)(2,1)} %get-tuple-element.7, bf16[4096,256]{1,0:T(8,128)(2,1)} %bitcast.3), kind=kOutput, calls=%fused_computation.161 | convolution fusion | flops 4294967296 | bytes 20971520 | tf_op jit(solution)/shard_map/dot_general | solution.py:66
  196.7 10.5 %fusion.73 = (bf16[2048,256]{1,0:T(8,128)(2,1)S(1)}, bf16[2048,256]{1,0:T(8,128)(2,1)}) fusion(bf16[2048,256]{1,0:T(8,128)(2,1)S(1)} %copy-done.23, f32[256]{0:T(256)S(1)} %copy-done.24, f32[2048,256]{1,0:T(8,128)} %fusion.83, bf16[256,256]{1,0:T(8,128)(2,1)S(1)} %copy-done.3, f32[2048,256]{1,0:T(8,128)} %fusion.85, f32[2048,256]{1,0:T(8,128)} %fusion.84, ...), kind=kOutput, calls=%fused_computation.127 | convolution fusion | flops 2431123456 | bytes 19006464 | tf_op jit(solution)/shard_map/dot_general | solution.py:69
  207.6 9.8 %convolution_convert_fusion = bf16[4096,256]{1,0:T(8,128)(2,1)} fusion(bf16[2048,4096]{1,0:T(8,128)(2,1)} %get-tuple-element.6, bf16[2048,256]{1,0:T(8,128)(2,1)S(1)} %fusion.70), kind=kOutput, calls=%fused_computation.106 | convolution fusion | flops 4296015872 | bytes 19922944 | tf_op jit(solution)/shard_map/dot_general | solution.py:24
  217.4 7.3 %all-to-all-start.2 = ((bf16[16,256,256]{2,1,0:T(8,128)(2,1)}), bf16[16,256,256]{2,1,0:T(8,128)(2,1)}, u32[]{:S(2)}, u32[]{:S(2)}) async-start(bf16[16,256,256]{2,1,0:T(8,128)(2,1)} %bitcast.34), calls=%async_computation.2 | async-start | bytes 4194304 | tf_op jit(solution)/shard_map/all_to_all | solution.py:90
  224.7 10.2 %fusion.87 = f32[4096,256]{1,0:T(8,128)} fusion(bf16[2048,4096]{1,0:T(8,128)(2,1)} %get-tuple-element.7, bf16[2048,256]{1,0:T(8,128)(2,1)S(1)} %fusion.70), kind=kOutput, calls=%fused_computation.163 | convolution fusion | flops 4294967296 | bytes 22020096 | tf_op jit(solution)/shard_map/dot_general | solution.py:24
  234.9 20.5 %all-to-all-done.2 = bf16[16,256,256]{2,1,0:T(8,128)(2,1)} async-done(((bf16[16,256,256]{2,1,0:T(8,128)(2,1)}), bf16[16,256,256]{2,1,0:T(8,128)(2,1)}, u32[]{:S(2)}, u32[]{:S(2)}) %all-to-all-start.2) | async-done | bytes 2097184 | tf_op jit(solution)/shard_map/all_to_all | solution.py:90
  255.4 8.1 %all-to-all-start.3 = ((f32[128,32,256]{2,1,0:T(8,128)}), f32[128,32,256]{2,1,0:T(8,128)}, u32[]{:S(2)}, u32[]{:S(2)}) async-start(f32[128,32,256]{2,1,0:T(8,128)} %bitcast.33), calls=%async_computation.3 | async-start | bytes 8388608 | tf_op jit(solution)/shard_map/all_to_all | solution.py:80
  263.5 6.0 %fusion.86 = f32[2048,256]{1,0:T(8,128)S(1)} fusion(bf16[2048,2048]{1,0:T(8,128)(2,1)} %fusion.54, bf16[2048,256]{1,0:T(8,128)(2,1)S(1)} %fusion.70), kind=kOutput, calls=%fused_computation.162 | convolution fusion | flops 2147483648 | bytes 11534336 | tf_op jit(solution)/shard_map/dot_general | solution.py:24
  270.1 8.7 %fusion.61 = f32[2048,256]{1,0:T(8,128)S(1)} fusion(f32[2048,256]{1,0:T(8,128)S(1)} %convolution_add_fusion, bf16[16,256,256]{2,1,0:T(8,128)(2,1)} %all-to-all-done.2, s32[16,256]{1,0:T(8,128)S(1)} %copy-done.18, pred[16,256]{1,0:T(8,128)(4,1)S(1)} %copy-done.20), kind=kOutput, calls=%fused_computation.110 | convolution fusion | flops 4312268800 | bytes 6311936 | tf_op jit(solution)/shard_map/dot_general | solution.py:24
  278.8 35.7 %all-to-all-done.3 = f32[128,32,256]{2,1,0:T(8,128)} async-done(((f32[128,32,256]{2,1,0:T(8,128)}), f32[128,32,256]{2,1,0:T(8,128)}, u32[]{:S(2)}, u32[]{:S(2)}) %all-to-all-start.3) | async-done | bytes 4194336 | tf_op jit(solution)/shard_map/all_to_all | solution.py:80
  314.5 2.5 reduce_sum.9
  317.0 1.5 scatter_fusion
  318.6 1.3 copy-done.17
  (63 shorter events, 4.1 us)
Async XLA Ops:
  0.6 2.8 copy-start
  1.4 0.8 copy-start.21
  2.1 0.6 copy-start.19
  12.6 8.8 %copy-start.4 = (s32[2048,16]{0,1:T(8,128)S(1)}, s32[2048,16]{0,1:T(8,128)}, u32[]{:S(2)}) copy-start(s32[2048,16]{0,1:T(8,128)} %param.13) | copy-start | bytes 393220
  14.2 116.8 %all-to-all-start = ((bf16[16,288,256]{2,1,0:T(8,128)(2,1)}), bf16[16,288,256]{2,1,0:T(8,128)(2,1)S(1)}, u32[]{:S(2)}, u32[]{:S(2)}) async-start(bf16[16,288,256]{2,1,0:T(8,128)(2,1)} %pad_maximum_fusion), calls=%async_computation | async-start | bytes 4718592 | tf_op jit(solution)/shard_map/all_to_all | solution.py:49
  21.8 0.6 copy-start.5
  21.8 0.6 copy-start.6
  21.8 0.6 copy-start.7
  21.8 0.6 copy-start.10
  21.8 0.6 copy-start.12
  21.9 0.6 copy-start.14
  21.9 0.6 copy-start.15
  131.0 41.8 %copy-start.2 = (bf16[256,256]{1,0:T(8,128)(2,1)S(1)}, bf16[256,256]{1,0:T(8,128)(2,1)}, u32[]{:S(2)}) copy-start(bf16[256,256]{1,0:T(8,128)(2,1)} %param.14) | copy-start | bytes 393220
  132.4 51.8 %all-to-all-start.1 = ((bf16[8,512,256]{2,1,0:T(8,128)(2,1)}), bf16[8,512,256]{2,1,0:T(8,128)(2,1)}, u32[]{:S(2)}, u32[]{:S(2)}) async-start(bf16[8,512,256]{2,1,0:T(8,128)(2,1)} %broadcast_in_dim.11), calls=%async_computation.1 | async-start | bytes 4194304 | tf_op jit(solution)/shard_map/all_to_all | solution.py:54
  184.2 12.5 %copy-start.3 = (bf16[256,256]{1,0:T(8,128)(2,1)S(1)}, bf16[256,256]{1,0:T(8,128)(2,1)}, u32[]{:S(2)}) copy-start(bf16[256,256]{1,0:T(8,128)(2,1)} %param.15) | copy-start | bytes 393220
  184.2 12.5 %copy-start.23 = (bf16[2048,256]{1,0:T(8,128)(2,1)S(1)}, bf16[2048,256]{1,0:T(8,128)(2,1)}, u32[]{:S(2)}) copy-start(bf16[2048,256]{1,0:T(8,128)(2,1)} %param.17) | copy-start | bytes 3145732
  184.2 12.5 %copy-start.24 = (f32[256]{0:T(256)S(1)}, f32[256]{0:T(256)}, u32[]{:S(2)}) copy-start(f32[256]{0:T(256)} %param.16) | copy-start | bytes 3076
  217.4 38.0 %all-to-all-start.2 = ((bf16[16,256,256]{2,1,0:T(8,128)(2,1)}), bf16[16,256,256]{2,1,0:T(8,128)(2,1)}, u32[]{:S(2)}, u32[]{:S(2)}) async-start(bf16[16,256,256]{2,1,0:T(8,128)(2,1)} %bitcast.34), calls=%async_computation.2 | async-start | bytes 4194304 | tf_op jit(solution)/shard_map/all_to_all | solution.py:90
  255.4 59.1 %all-to-all-start.3 = ((f32[128,32,256]{2,1,0:T(8,128)}), f32[128,32,256]{2,1,0:T(8,128)}, u32[]{:S(2)}, u32[]{:S(2)}) async-start(f32[128,32,256]{2,1,0:T(8,128)} %bitcast.33), calls=%async_computation.3 | async-start | bytes 8388608 | tf_op jit(solution)/shard_map/all_to_all | solution.py:80
  263.5 6.5 %copy-start.18 = (s32[16,256]{1,0:T(8,128)S(1)}, s32[16,256]{1,0:T(8,128)}, u32[]{:S(2)}) copy-start(s32[16,256]{1,0:T(8,128)} %param.10) | copy-start | bytes 49156
  263.5 6.5 %copy-start.20 = (pred[16,256]{1,0:T(8,128)(4,1)S(1)}, pred[16,256]{1,0:T(8,128)(4,1)}, u32[]{:S(2)}) copy-start(pred[16,256]{1,0:T(8,128)(4,1)} %copy-done.19) | copy-start | bytes 12292
  270.0 47.0 %copy-start.22 = (s32[32]{0:T(128)S(1)}, s32[32]{0:T(128)}, u32[]{:S(2)}) copy-start(s32[32]{0:T(128)} %copy-done.21) | copy-start | bytes 388
  270.0 49.8 %copy-start.1 = (bf16[2048,256]{1,0:T(8,128)(2,1)S(1)}, bf16[2048,256]{1,0:T(8,128)(2,1)}, u32[]{:S(2)}) copy-start(bf16[2048,256]{1,0:T(8,128)(2,1)} %param.9) | copy-start | bytes 3145732
  318.6 1.3 copy-start.17
  (5 other events, 2.9 us)

commit v6 on v5

--- a/solution.py
+++ b/solution.py
@@ -54,16 +54,14 @@
     hub_table = lax.all_to_all(hub_copies, "row", split_axis=0, concat_axis=0, tiled=True)
     hub_table = hub_table.reshape(device_count * hub_count, feature_width)
 
-    counts_own = count_matrix(neighbours, 0, vertex_count)
-    counts_halo = count_matrix(neighbours, vertex_count, halo_width)
-    counts_hub = count_matrix(neighbours, hub_start, device_count * hub_count)
-    counts_own, counts_halo, counts_hub = lax.optimization_barrier(
-        (counts_own, counts_halo, counts_hub)
-    )
+    source_table = jnp.concatenate([features, incoming, hub_table], axis=0)
+    half = source_table.shape[0] // 2
+    counts_low = count_matrix(neighbours, 0, half)
+    counts_high = count_matrix(neighbours, half, half)
+    counts_low, counts_high = lax.optimization_barrier((counts_low, counts_high))
 
-    summed = jnp.dot(counts_own, features, preferred_element_type=jnp.float32)
-    summed = summed + jnp.dot(counts_halo, incoming, preferred_element_type=jnp.float32)
-    summed = summed + jnp.dot(counts_hub, hub_table, preferred_element_type=jnp.float32)
+    summed = jnp.dot(counts_low, source_table[:half], preferred_element_type=jnp.float32)
+    summed = summed + jnp.dot(counts_high, source_table[half:], preferred_element_type=jnp.float32)
     aggregated = (summed * (1.0 / degree)).astype(jnp.bfloat16)
     preact = jnp.dot(features, w_self, preferred_element_type=jnp.float32)
     preact = preact + jnp.dot(aggregated, w_neigh, preferred_element_type=jnp.float32) + bias_vector
@@ -76,7 +74,10 @@
     )
     scaled_grads = (grad_aggregated.astype(jnp.float32) * (1.0 / degree)).astype(jnp.bfloat16)
 
-    hub_back = transposed_dot(counts_hub, scaled_grads)
+    back_low = transposed_dot(counts_low, scaled_grads)
+    back_high = transposed_dot(counts_high, scaled_grads)
+    table_grads = jnp.concatenate([back_low, back_high], axis=0)
+    hub_back = table_grads[hub_start:]
     hub_parts = lax.all_to_all(
         hub_back.reshape(device_count, hub_count, feature_width),
         ("row", "col"),
@@ -86,7 +87,7 @@
     )
     hub_owned = jnp.sum(hub_parts, axis=0)
 
-    halo_back = transposed_dot(counts_halo, scaled_grads)
+    halo_back = table_grads[vertex_count:hub_start]
     returned = lax.all_to_all(
         halo_back.astype(jnp.bfloat16).reshape(peer_count, slot_count, feature_width),
         "col",
@@ -94,7 +95,7 @@
         concat_axis=0,
         tiled=True,
     )
-    grad_rows = grad_direct + transposed_dot(counts_own, scaled_grads)
+    grad_rows = grad_direct + table_grads[:vertex_count]
     grad_rows = grad_rows + transposed_dot(picks, returned.reshape(halo_width, feature_width))
     grad_rows = grad_rows.at[hub_rows].add(hub_owned)
     return (output_rows, grad_rows)

time: 322 us -> 337 us (1.047)
  waiting for transfers between devices: 56.2 us -> 76.5 us
  matrix products: 78.3 us -> 71.3 us
  local copies, waits for them, and re-layouts: 5.84 us -> 12.6 us
    all_to_all x1, waiting for transfers between devices: 0.01 us -> 10.9 us  [local(): lax.all_to_all(hub_copies, 'row', split_axis=0, concat_axis=0, tiled=True)]
    dot_general x2 -> x1, matrix products: 21.9 us -> 12.3 us  [local(): jnp.dot(counts_low, source_table[:half], preferred_element_type=jnp.float32)]
    add x2 -> x1, other arithmetic: 144 us -> 137 us  [count_matrix(): counts + (narrow_rows[:, slot:slot + 1] == column_ids[None, :]).astype(jn...]
    all_to_all x1, waiting for transfers between devices: 20.5 us -> 25.4 us  [local(): lax.all_to_all(halo_back.astype(jnp.bfloat16).reshape(peer_count, slot_co...]
    all_to_all x1, waiting for transfers between devices: 35.7 us -> 40.2 us  [local(): lax.all_to_all(hub_back.reshape(device_count, hub_count, feature_width),...]
    slice x0 -> x1, local copies, waits for them, and re-layouts: none -> 4.47 us  [local(): hub_back = table_grads[hub_start:]]
    dot_general x1, matrix products: 10.5 us -> 13.8 us  [local(): jnp.dot(aggregated, w_neigh, preferred_element_type=jnp.float32)]
    dot_general x4 -> x3, matrix products: 34.8 us -> 31.4 us  [transposed_dot(): lax.dot_general(counts, values, (((0,), (0,)), ((), ())), preferred_eleme...]
  transfers between devices with their start and end apart: 4 -> 4, of which waited for: 2 -> 3; matrix products, arithmetic and copies ran while one was open for 57% -> 50% of each run, Pallas kernels for 0% -> 0%
where the time goes in v6:
time: 337 us; the launch traced here: 335 us
  other arithmetic  148 us (44%)
  waiting for transfers between devices  76.5 us (23%)
  matrix products  71.3 us (21%)
  starting transfers between devices  25.7 us (8%)
  local copies, waits for them, and re-layouts  12.6 us (4%)
    add x1, other arithmetic, count_matrix(): counts + (narrow_rows[:, slot:slot + 1] == column_ids[None, :]).astype(jn...  137 us
    all_to_all x1, waiting for transfers between devices, local(): lax.all_to_all(hub_back.reshape(device_count, hub_count, feature_width),...  40.2 us
    dot_general x3, matrix products, transposed_dot(): lax.dot_general(counts, values, (((0,), (0,)), ((), ())), preferred_eleme...  31.4 us
    all_to_all x1, waiting for transfers between devices, local(): lax.all_to_all(halo_back.astype(jnp.bfloat16).reshape(peer_count, slot_co...  25.4 us
    dot_general x1, matrix products, local(): jnp.dot(aggregated, w_neigh, preferred_element_type=jnp.float32)  13.8 us
    dot_general x1, matrix products, local(): jnp.dot(counts_low, source_table[:half], preferred_element_type=jnp.float32)  12.3 us
    all_to_all x1, waiting for transfers between devices, local(): lax.all_to_all(hub_copies, 'row', split_axis=0, concat_axis=0, tiled=True)  10.9 us
    dot_general x1, matrix products, local(): jnp.dot(picks, features, preferred_element_type=jnp.float32)  8.55 us
  transfers between devices with their start and end apart: 4, of which 3 were waited for; matrix products, arithmetic and copies ran while one was open for 50% of the time, Pallas kernels for 0%

profile of v6, /device:TPU:0, one launch (start us, length us, event | category | flops | bytes accessed | tf_op | source)
XLA Modules:
  0.0 334.5 jit_solution(5731095517380277489)
XLA Ops:
  2.8 2.0 gather_fusion
  4.8 8.5 %fusion.40 = bf16[4096,256]{1,0:T(8,128)(2,1)S(1)} fusion(bf16[2048,256]{1,0:T(8,128)(2,1)} %param.9, s32[4096]{0:T(1024)S(1)} %bitcast.35, pred[4096]{0:T(1024)(128)(4,1)S(1)} %lt.28), kind=kOutput, calls=%fused_computation.74 | convolution fusion | flops 4312793088 | bytes 3166208 | tf_op jit(solution)/shard_map/dot_general | solution.py:44
  13.4 1.7 pad_maximum_fusion.6
  15.0 7.1 %all-to-all-start = ((bf16[16,288,256]{2,1,0:T(8,128)(2,1)}), bf16[16,288,256]{2,1,0:T(8,128)(2,1)S(1)}, u32[]{:S(2)}, u32[]{:S(2)}) async-start(bf16[16,288,256]{2,1,0:T(8,128)(2,1)} %pad_maximum_fusion.6), calls=%async_computation | async-start | bytes 4718592 | tf_op jit(solution)/shard_map/all_to_all | solution.py:49
  22.6 137.4 %fusion.35 = (bf16[2048,5120]{1,0:T(8,128)(2,1)}, bf16[2048,5120]{1,0:T(8,128)(2,1)}) fusion(s16[5120]{0:T(1024)(128)(2,1)S(1)} %iota_add_fusion, s16[2048]{0:T(1024)(128)(2,1)S(1)} %get-tuple-element.7, s16[2048]{0:T(1024)(128)(2,1)S(1)} %get-tuple-element.8, s16[2048]{0:T(1024)(128)(2,1)S(1)} %get-tuple-element.9, ...), kind=kLoop, calls=%fused_computation.69 | loop fusion | flops 1342177280 | bytes 42018816 | tf_op jit(solution)/shard_map/add | solution.py:17
  160.1 1.5 broadcast_in_dim.11
  161.6 5.3 %all-to-all-start.1 = ((bf16[8,512,256]{2,1,0:T(8,128)(2,1)}), bf16[8,512,256]{2,1,0:T(8,128)(2,1)}, u32[]{:S(2)}, u32[]{:S(2)}) async-start(bf16[8,512,256]{2,1,0:T(8,128)(2,1)} %broadcast_in_dim.11), calls=%async_computation.1 | async-start | bytes 4194304 | tf_op jit(solution)/shard_map/all_to_all | solution.py:54
  166.9 2.7 fusion.74
  171.0 12.3 %fusion.52 = f32[2048,256]{1,0:T(8,128)} fusion(bf16[2048,5120]{1,0:T(8,128)(2,1)} %get-tuple-element.4, bf16[4096,256]{1,0:T(8,128)(2,1)S(1)} %bitcast.30, bf16[2048,256]{1,0:T(8,128)(2,1)S(1)} %copy-done.3), kind=kOutput, calls=%fused_computation.89 | convolution fusion | flops 5373952000 | bytes 26214400 | tf_op jit(solution)/shard_map/dot_general | solution.py:63
  183.3 10.9 %all-to-all-done.1 = bf16[8,512,256]{2,1,0:T(8,128)(2,1)} async-done(((bf16[8,512,256]{2,1,0:T(8,128)(2,1)}), bf16[8,512,256]{2,1,0:T(8,128)(2,1)}, u32[]{:S(2)}, u32[]{:S(2)}) %all-to-all-start.1) | async-done | bytes 2097184 | tf_op jit(solution)/shard_map/all_to_all | solution.py:54
  194.2 13.8 %fusion.60 = (bf16[2048,256]{1,0:T(8,128)(2,1)S(1)}, bf16[2048,256]{1,0:T(8,128)(2,1)}) fusion(bf16[2048,256]{1,0:T(8,128)(2,1)} %param.17, f32[256]{0:T(256)S(1)} %copy-done.8, f32[2048,256]{1,0:T(8,128)} %fusion.74, bf16[256,256]{1,0:T(8,128)(2,1)S(1)} %copy-done, f32[2048,256]{1,0:T(8,128)} %fusion.52, bf16[2048,5120]{1,0:T(8,128)(2,1)} %get-tuple-element.5, ...), kind=kOutput, calls=%fused_computation.99 | convolution fusion | flops 5657067520 | bytes 32637952 | tf_op jit(solution)/shard_map/dot_general | solution.py:67
  208.5 14.2 %fusion.73 = (bf16[5120,256]{1,0:T(8,128)(2,1)}, f32[5120,256]{1,0:T(8,128)}) fusion(bf16[2048,5120]{1,0:T(8,128)(2,1)} %get-tuple-element.4, bf16[2048,256]{1,0:T(8,128)(2,1)S(1)} %fusion.57), kind=kOutput, calls=%fused_computation.133 | convolution fusion | flops 5370019840 | bytes 29884416 | tf_op jit(solution)/shard_map/dot_general | solution.py:24
  223.5 8.5 %fusion.72 = (bf16[5120,256]{1,0:T(8,128)(2,1)}, f32[5120,256]{1,0:T(8,128)}) fusion(bf16[2048,5120]{1,0:T(8,128)(2,1)S(1)} %bitcast.28, bf16[2048,256]{1,0:T(8,128)(2,1)S(1)} %fusion.57), kind=kOutput, calls=%fused_computation.132 | convolution fusion | flops 5370019840 | bytes 29884416 | tf_op jit(solution)/shard_map/dot_general | solution.py:24
  232.0 3.0 pad_maximum_fusion.7
  235.0 7.4 %all-to-all-start.2 = ((bf16[16,256,256]{2,1,0:T(8,128)(2,1)}), bf16[16,256,256]{2,1,0:T(8,128)(2,1)}, u32[]{:S(2)}, u32[]{:S(2)}) async-start(bf16[16,256,256]{2,1,0:T(8,128)(2,1)} %bitcast.4), calls=%async_computation.2 | async-start | bytes 4194304 | tf_op jit(solution)/shard_map/all_to_all | solution.py:91
  242.4 4.5 %slice.132 = f32[4096,256]{1,0:T(8,128)} slice(f32[5120,256]{1,0:T(8,128)} %get-tuple-element.27), slice={[1024:5120], [0:256]} | slice | bytes 8388608 | tf_op jit(solution)/shard_map/slice | solution.py:80
  246.9 25.4 %all-to-all-done.2 = bf16[16,256,256]{2,1,0:T(8,128)(2,1)} async-done(((bf16[16,256,256]{2,1,0:T(8,128)(2,1)}), bf16[16,256,256]{2,1,0:T(8,128)(2,1)}, u32[]{:S(2)}, u32[]{:S(2)}) %all-to-all-start.2) | async-done | bytes 2097184 | tf_op jit(solution)/shard_map/all_to_all | solution.py:91
  272.3 5.8 %all-to-all-start.3 = ((f32[128,32,256]{2,1,0:T(8,128)}), f32[128,32,256]{2,1,0:T(8,128)}, u32[]{:S(2)}, u32[]{:S(2)}) async-start(f32[128,32,256]{2,1,0:T(8,128)} %bitcast.29), calls=%async_computation.3 | async-start | bytes 8388608 | tf_op jit(solution)/shard_map/all_to_all | solution.py:81
  278.2 2.1 convolution_add_fusion
  280.3 8.7 %fusion.46 = f32[2048,256]{1,0:T(8,128)S(1)} fusion(f32[2048,256]{1,0:T(8,128)S(1)} %convolution_add_fusion, bf16[16,256,256]{2,1,0:T(8,128)(2,1)} %all-to-all-done.2, s32[16,256]{1,0:T(8,128)S(1)} %copy-done.7, pred[16,256]{1,0:T(8,128)(4,1)S(1)} %iota_compare_fusion.2), kind=kOutput, calls=%fused_computation.78 | convolution fusion | flops 4312268800 | bytes 6311936 | tf_op jit(solution)/shard_map/dot_general | solution.py:24
  289.0 40.2 %all-to-all-done.3 = f32[128,32,256]{2,1,0:T(8,128)} async-done(((f32[128,32,256]{2,1,0:T(8,128)}), f32[128,32,256]{2,1,0:T(8,128)}, u32[]{:S(2)}, u32[]{:S(2)}) %all-to-all-start.3) | async-done | bytes 4194336 | tf_op jit(solution)/shard_map/all_to_all | solution.py:81
  329.2 2.5 reduce_sum.9
  331.7 1.5 scatter_fusion
  333.2 1.3 copy-done.6
  (41 shorter events, 5.2 us)
Async XLA Ops:
  0.6 193.5 %copy-start = (bf16[256,256]{1,0:T(8,128)(2,1)S(1)}, bf16[256,256]{1,0:T(8,128)(2,1)}, u32[]{:S(2)}) copy-start(bf16[256,256]{1,0:T(8,128)(2,1)} %param.15) | copy-start | bytes 393220
  4.8 17.4 %copy-start.5 = (s32[2048,16]{0,1:T(8,128)S(1)}, s32[2048,16]{0,1:T(8,128)}, u32[]{:S(2)}) copy-start(s32[2048,16]{0,1:T(8,128)} %param.13) | copy-start | bytes 393220
  15.0 145.0 %all-to-all-start = ((bf16[16,288,256]{2,1,0:T(8,128)(2,1)}), bf16[16,288,256]{2,1,0:T(8,128)(2,1)S(1)}, u32[]{:S(2)}, u32[]{:S(2)}) async-start(bf16[16,288,256]{2,1,0:T(8,128)(2,1)} %pad_maximum_fusion.6), calls=%async_computation | async-start | bytes 4718592 | tf_op jit(solution)/shard_map/all_to_all | solution.py:49
  22.6 144.3 %copy-start.3 = (bf16[2048,256]{1,0:T(8,128)(2,1)S(1)}, bf16[2048,256]{1,0:T(8,128)(2,1)}, u32[]{:S(2)}) copy-start(bf16[2048,256]{1,0:T(8,128)(2,1)} %param.9) | copy-start | bytes 3145732
  161.6 32.6 %all-to-all-start.1 = ((bf16[8,512,256]{2,1,0:T(8,128)(2,1)}), bf16[8,512,256]{2,1,0:T(8,128)(2,1)}, u32[]{:S(2)}, u32[]{:S(2)}) async-start(bf16[8,512,256]{2,1,0:T(8,128)(2,1)} %broadcast_in_dim.11), calls=%async_computation.1 | async-start | bytes 4194304 | tf_op jit(solution)/shard_map/all_to_all | solution.py:54
  169.7 1.3 copy-start.2
  171.0 23.2 %copy-start.8 = (f32[256]{0:T(256)S(1)}, f32[256]{0:T(256)}, u32[]{:S(2)}) copy-start(f32[256]{0:T(256)} %param.16) | copy-start | bytes 3076
  208.0 14.7 %slice-start = ((s8[20971520]{0:T(1024)(128)(4,1)}), s8[4194304]{0:T(1024)(128)(4,1)S(1)}, s32[]{:S(2)}) async-start(s8[20971520]{0:T(1024)(128)(4,1)} %bitcast.27), calls=%async_computation.4 | async-start | bytes 8388608
  208.5 14.3 %slice-start.1 = ((s8[20971520]{0:T(1024)(128)(4,1)}), s8[4194304]{0:T(1024)(128)(4,1)S(1)}, s32[]{:S(2)}) async-start(s8[20971520]{0:T(1024)(128)(4,1)} %bitcast.27), calls=%async_computation.5 | async-start | bytes 8388608
  208.5 14.2 %slice-start.2 = ((s8[20971520]{0:T(1024)(128)(4,1)}), s8[4194304]{0:T(1024)(128)(4,1)S(1)}, s32[]{:S(2)}) async-start(s8[20971520]{0:T(1024)(128)(4,1)} %bitcast.27), calls=%async_computation.6 | async-start | bytes 8388608
  208.5 14.2 %slice-start.3 = ((s8[20971520]{0:T(1024)(128)(4,1)}), s8[4194304]{0:T(1024)(128)(4,1)S(1)}, s32[]{:S(2)}) async-start(s8[20971520]{0:T(1024)(128)(4,1)} %bitcast.27), calls=%async_computation.7 | async-start | bytes 8388608
  208.5 14.9 %slice-start.4 = ((s8[20971520]{0:T(1024)(128)(4,1)}), s8[4194304]{0:T(1024)(128)(4,1)S(1)}, s32[]{:S(2)}) async-start(s8[20971520]{0:T(1024)(128)(4,1)} %bitcast.27), calls=%async_computation.8 | async-start | bytes 8388608
  235.0 43.1 %copy-start.4 = (bf16[256,256]{1,0:T(8,128)(2,1)S(1)}, bf16[256,256]{1,0:T(8,128)(2,1)}, u32[]{:S(2)}) copy-start(bf16[256,256]{1,0:T(8,128)(2,1)} %param.14) | copy-start | bytes 393220
  235.0 37.3 %all-to-all-start.2 = ((bf16[16,256,256]{2,1,0:T(8,128)(2,1)}), bf16[16,256,256]{2,1,0:T(8,128)(2,1)}, u32[]{:S(2)}, u32[]{:S(2)}) async-start(bf16[16,256,256]{2,1,0:T(8,128)(2,1)} %bitcast.4), calls=%async_computation.2 | async-start | bytes 4194304 | tf_op jit(solution)/shard_map/all_to_all | solution.py:91
  242.4 37.8 %copy-start.7 = (s32[16,256]{1,0:T(8,128)S(1)}, s32[16,256]{1,0:T(8,128)}, u32[]{:S(2)}) copy-start(s32[16,256]{1,0:T(8,128)} %param.10) | copy-start | bytes 49156
  272.3 56.9 %all-to-all-start.3 = ((f32[128,32,256]{2,1,0:T(8,128)}), f32[128,32,256]{2,1,0:T(8,128)}, u32[]{:S(2)}, u32[]{:S(2)}) async-start(f32[128,32,256]{2,1,0:T(8,128)} %bitcast.29), calls=%async_computation.3 | async-start | bytes 8388608 | tf_op jit(solution)/shard_map/all_to_all | solution.py:81
  280.3 54.3 %copy-start.1 = (bf16[256,256]{1,0:T(8,128)(2,1)S(1)}, bf16[256,256]{1,0:T(8,128)(2,1)}, u32[]{:S(2)}) copy-start(bf16[256,256]{1,0:T(8,128)(2,1)} %param.15) | copy-start | bytes 393220
  333.2 1.3 copy-start.6
